TPU v7x, 256 devices: a whole 4x4x8 slice. The times are simulated.
256 devices in a mesh: ex: 4 (over x), row: 8 (over y, core), col: 8 (over z).
Axes of the slice: x: 4, y: 4, z: 8, core: 2. Of those that a mesh axis runs over, the one named last changes fastest.
Arguments:
- inputs: bfloat16 [32, 256, 256, 128], P('ex', 'row', 'col'), may hold values from -6 to 6
- cotangent: bfloat16 [32, 256, 256, 128], P('ex', 'row', 'col'), may hold values from -200 to 200, as said below
- weight: bfloat16 [3, 3, 128, 128], replicated, may hold values from -0.1875 to 0.1875
- bias: float32 [128], replicated, may hold values from -1 to 1
- noise_weight: float32 [1152, 128], P(('row', 'col')), may hold values from -6 to 6
- noise_bias: float32 [128], replicated, may hold values from -6 to 6
Outputs:
- input_grad: bfloat16 [32, 256, 256, 128], P('ex', 'row', 'col')
- grad_weight: float32 [1152, 128], P(('row', 'col'))
- grad_bias: float32 [128], replicated
Inputs may be any that keep to these rules, and one draw needn't show every extreme that they name: Each example's cotangent has its own overall scale.
All inputs are finite; a program needn't handle non-finite values.
Results may differ from a plain program's by a relative error of at most 0.0055.
Values may be sent and summed in bfloat16 or wider, within the bound.
A program may use at most 64 MiB of HBM per device.

v0:
```python
import math

import jax
import jax.numpy as jnp
from jax import lax
from jax.sharding import PartitionSpec as P

noise_multiplier = 0.002
epsilon = 1e-06


def with_halo(block, sides, width):
    for axis, dim in sides:
        count = lax.axis_size(axis)
        forward = [(i, i + 1) for i in range(count - 1)]
        backward = [(target, source) for source, target in forward]
        low = lax.ppermute(
            lax.slice_in_dim(block, block.shape[dim] - width, None, axis=dim), axis, forward
        )
        high = lax.ppermute(lax.slice_in_dim(block, 0, width, axis=dim), axis, backward)
        block = jnp.concatenate([low, block, high], axis=dim)
    return block


def local(inputs, cotangent, weight, bias, noise_weight, noise_bias):
    examples, tile_rows, tile_cols, channels = inputs.shape
    padded = with_halo(inputs, (("row", 1), ("col", 2)), 1)
    preact = bias
    for tap_row in range(3):
        for tap_col in range(3):
            window = padded[
                :, tap_row : tap_row + tile_rows, tap_col : tap_col + tile_cols
            ].reshape(-1, channels)
            preact = preact + jnp.dot(
                window, weight[tap_row, tap_col], preferred_element_type=jnp.float32
            )
    sigmoid_z = jax.nn.sigmoid(preact)
    slope = sigmoid_z * (1.0 + preact * (1.0 - sigmoid_z))
    grad_z = (cotangent.reshape(-1, channels).astype(jnp.float32) * slope).astype(jnp.bfloat16)
    grad_tile = grad_z.reshape(examples, tile_rows, tile_cols, channels)
    grad_pad = with_halo(grad_tile, (("row", 1), ("col", 2)), 1)
    backward = jnp.zeros((examples * tile_rows * tile_cols, channels), jnp.float32)
    flat_grad = grad_z.reshape(examples, tile_rows * tile_cols, channels)
    pieces = []
    for tap_row in range(3):
        for tap_col in range(3):
            shifted = grad_pad[
                :, 2 - tap_row : 2 - tap_row + tile_rows, 2 - tap_col : 2 - tap_col + tile_cols
            ].reshape(-1, channels)
            backward = backward + jnp.dot(
                shifted, weight[tap_row, tap_col].T, preferred_element_type=jnp.float32
            )
            window = padded[
                :, tap_row : tap_row + tile_rows, tap_col : tap_col + tile_cols
            ].reshape(examples, -1, channels)
            pieces.append(
                jnp.einsum("nkc,nkd->cnd", window, flat_grad, preferred_element_type=jnp.float32)
            )
    input_grad = backward.astype(jnp.bfloat16).reshape(examples, tile_rows, tile_cols, channels)
    partial_value = jnp.stack(pieces).reshape(9 * channels, examples, channels)
    bias_part = jnp.sum(flat_grad.astype(jnp.float32), axis=1)
    height = tile_rows * lax.axis_size("row")
    width = tile_cols * lax.axis_size("col")
    clip = math.sqrt(height * width * 9 * channels * channels)
    groups = lax.axis_size(("row", "col"))
    share_rows = 9 * channels // groups
    summed, bias_sum = lax.psum((partial_value, bias_part), ("row", "col"))
    squares = jnp.sum(summed * summed, axis=(0, 2)) + jnp.sum(bias_sum * bias_sum, axis=1)
    start_row = lax.axis_index(("row", "col")) * share_rows
    owned = lax.dynamic_slice_in_dim(summed, start_row, share_rows, 0)
    factor = jnp.minimum(1.0, clip / jnp.sqrt(squares + epsilon))
    weighted = jnp.sum(owned * factor[None, :, None], axis=1)
    bias_weighted = jnp.sum(bias_sum * factor[:, None], axis=0)
    total_weight, total_bias = lax.psum((weighted, bias_weighted), "ex")
    scale = 1.0 / math.sqrt(examples * lax.axis_size("ex") * height * width)
    grad_weight = (total_weight + noise_multiplier * clip * noise_weight) * scale
    grad_bias = (total_bias + noise_multiplier * clip * noise_bias) * scale
    return (input_grad, grad_weight, grad_bias)


def solution(mesh):
    in_specs = (
        P("ex", "row", "col", None),
        P("ex", "row", "col", None),
        P(),
        P(),
        P(("row", "col"), None),
        P(),
    )
    out_specs = (P("ex", "row", "col", None), P(("row", "col"), None), P())
    return jax.shard_map(local, mesh=mesh, in_specs=in_specs, out_specs=out_specs, check_vma=False)
```

profile of v0, /device:TPU:1, one launch (start us, length us, event | category | flops | bytes accessed | tf_op | source)
XLA Modules:
  0.0 286.8 jit_solution(14727578206730465073)
XLA Ops:
  7.2 0.9 fusion.64
  8.1 4.6 %collective-permute-start = (bf16[8,1,32,128]{3,2,1,0:T(8,128)(2,1)S(1)}, bf16[8,1,32,128]{3,2,1,0:T(8,128)(2,1)S(1)}, u32[]{:S(2)}, u32[]{:S(2)}) collective-permute-start(bf16[8,1,32,128]{3,2,1,0:T(8,128)(2,1)S(1)} %get-tuple-element.34), channel_id=1, source_target_pairs={{0,8},{8,16},{16,24},{24,32},{32,40},{40,48},{48,56},{1,9},{9,17},... | collective-permute-start | bytes 196616 | tf_op jit(solution)/shard_map/ppermute | solution.py:17
  12.7 1.9 collective-permute-start.1
  14.7 3.6 %collective-permute-done.1 = bf16[8,1,32,128]{3,2,1,0:T(8,128)(2,1)S(1)} collective-permute-done((bf16[8,1,32,128]{3,2,1,0:T(8,128)(2,1)S(1)}, bf16[8,1,32,128]{3,2,1,0:T(8,128)(2,1)S(1)}, u32[]{:S(2)}, u32[]{:S(2)}) %collective-permute-start.1) | collective-permute-done | bytes 65568 | tf_op jit(solution)/shard_map/ppermute | solution.py:20
  18.3 3.7 %pad_maximum_fusion.6 = (bf16[8,32,32,128]{3,2,1,0:T(8,128)(2,1)S(1)}, bf16[8,32,32,128]{3,2,1,0:T(8,128)(2,1)S(1)}, bf16[8,34,32,128]{3,2,1,0:T(8,128)(2,1)S(1)}) fusion(bf16[8,32,32,128]{3,2,1,0:T(8,128)(2,1)} %param.6, bf16[8,1,32,128]{3,2,1,0:T(8,128)(2,1)S(1)} %collective-permute-done, bf16[8,1,32,128]{3,2,1,0:T(8,128)(2,1)S(1)} %collective-permute-done.1, ...), kind=kLoop, calls=%fused_computation.41 | loop fusion | flops 8388608 | bytes 8519680 | tf_op jit(solution)/shard_map/concatenate | solution.py:21
  22.2 3.5 %collective-permute-start.2 = (bf16[8,34,1,128]{3,2,1,0:T(2,128)(2,1)S(1)}, bf16[8,34,1,128]{3,2,1,0:T(2,128)(2,1)S(1)}, u32[]{:S(2)}, u32[]{:S(2)}) collective-permute-start(bf16[8,34,1,128]{3,2,1,0:T(2,128)(2,1)S(1)} %get-tuple-element.24), channel_id=1, source_target_pairs={{0,1},{1,2},{2,3},{3,4},{4,5},{5,6},{6,7},{8,9},{9,10},{10,11},{11... | collective-permute-start | bytes 208904 | tf_op jit(solution)/shard_map/ppermute | solution.py:17
  25.8 1.3 collective-permute-start.3
  27.8 4.0 %collective-permute-done.3 = bf16[8,34,1,128]{3,2,1,0:T(2,128)(2,1)S(1)} collective-permute-done((bf16[8,34,1,128]{3,2,1,0:T(2,128)(2,1)S(1)}, bf16[8,34,1,128]{3,2,1,0:T(2,128)(2,1)S(1)}, u32[]{:S(2)}, u32[]{:S(2)}) %collective-permute-start.3) | collective-permute-done | bytes 69664 | tf_op jit(solution)/shard_map/ppermute | solution.py:20
  31.8 7.2 %pad_maximum_fusion.5 = (bf16[8,32,32,128]{3,2,1,0:T(8,128)(2,1)}, bf16[8,32,32,128]{3,2,1,0:T(8,128)(2,1)S(1)}, bf16[8,32,32,128]{3,2,1,0:T(8,128)(2,1)S(1)}, b...) fusion(bf16[8,34,32,128]{3,2,1,0:T(8,128)(2,1)S(1)} %constant_dyna, ...), kind=kLoop, calls=%fused_computation.40 | loop fusion | flops 25165824 | bytes 14950400 | tf_op jit(solution)/shard_map/concatenate | solution.py:21
  44.9 4.6 %convert_reduce_fusion = (f32[8,128]{1,0:T(8,128)S(1)}, bf16[8192,128]{1,0:T(8,128)(2,1)S(1)}) fusion(f32[8192,128]{1,0:T(8,128)S(1)} %fusion.21, f32[8192,128]{1,0:T(8,128)S(1)} %fusion.24, f32[8192,128]{1,0:T(8,128)S(1)} %convolution_add_fusion.8, bf16[8192,128]{1,0:T(8,128)(2,1)} %bitcast.208, bf16[3,3,128,128]{3,2,1,0:T(8,128)(2,1)S(1)} %copy-done.2, ...), kind=kOutput, calls=%fused_computation.21 | convolution fusion | flops 284163072 | bytes 18911232 | tf_op jit(solution)/shard_map/dot_general | solution.py:34
  55.8 1.0 fusion.11
  57.5 4.9 %copy.37 = f32[9,128,8,128]{3,2,1,0:T(8,128)} copy(f32[9,128,8,128]{3,1,2,0:T(8,128)S(1)} %fusion.10) | data formatting | bytes 9437184 | tf_op jit(solution)/shard_map/stack | solution.py:60
  62.4 117.6 %psum.29 = f32[8,128]{1,0:T(8,128)S(1)} all-reduce(f32[8,128]{1,0:T(8,128)S(1)} %get-tuple-element.35), channel_id=1, replica_groups=mesh['ex'=4,'row'=8,'col'=8] {'row','col'}, use_global_device_ids=true, to_apply=%region_3.0 | all-reduce | flops 1024 | bytes 8192 | tf_op jit(solution)/shard_map/psum | solution.py:67
  180.0 1.9 collective-permute-start.4
  182.0 10.3 %collective-permute-start.5 = (bf16[8,1,32,128]{3,2,1,0:T(8,128)(2,1)S(1)}, bf16[8,1,32,128]{3,2,1,0:T(8,128)(2,1)S(1)}, u32[]{:S(2)}, u32[]{:S(2)}) collective-permute-start(bf16[8,1,32,128]{3,2,1,0:T(8,128)(2,1)S(1)} %get-tuple-element.29), channel_id=1, source_target_pairs={{8,0},{16,8},{24,16},{32,24},{40,32},{48,40},{56,48},{9,1},{17,9},... | collective-permute-start | bytes 196616 | tf_op jit(solution)/shard_map/ppermute | solution.py:20
  193.4 1.3 collective-permute-start.6
  194.7 4.0 %collective-permute-start.7 = (bf16[8,34,1,128]{3,2,1,0:T(2,128)(2,1)S(1)}, bf16[8,34,1,128]{3,2,1,0:T(2,128)(2,1)S(1)}, u32[]{:S(2)}, u32[]{:S(2)}) collective-permute-start(bf16[8,34,1,128]{3,2,1,0:T(2,128)(2,1)S(1)} %get-tuple-element.20), channel_id=1, source_target_pairs={{0,1},{1,2},{2,3},{3,4},{4,5},{5,6},{6,7},{8,9},{9,10},{10,11},{11... | collective-permute-start | bytes 208904 | tf_op jit(solution)/shard_map/ppermute | solution.py:17
  201.1 1.7 pad_maximum_fusion
  202.9 1.4 fusion.60
  210.2 2.1 fusion.4
  212.3 49.2 %all-reduce.3.cloned.1.call-done = f32[1152,8,128]{2,1,0:T(8,128)} async-done(((f32[1152,8,128]{2,1,0:T(8,128)}), f32[1152,8,128]{2,1,0:T(8,128)}) %all-reduce.3.cloned.1.call-update) | async-done | bytes 4718608 | tf_op jit(solution)/shard_map/psum | solution.py:67
  261.5 3.1 %multiply_reduce_fusion = f32[8]{0:T(128)S(1)} fusion(f32[1152,8,128]{2,1,0:T(8,128)} %all-reduce.3.cloned.1.call-done), kind=kLoop, calls=%fused_computation.18 | loop fusion | flops 2359288 | bytes 4718624 | tf_op jit(solution)/shard_map/reduce_sum | solution.py:68
  264.7 1.0 multiply_reduce_fusion.1
  265.7 13.1 %all-reduce = (f32[18,128]{1,0:T(8,128)S(1)}, f32[128]{0:T(128)S(1)}) all-reduce(f32[18,128]{1,0:T(8,128)S(1)} %multiply_reduce_fusion.1, f32[128]{0:T(128)S(1)} %multiply_reduce_fusion.2), channel_id=1, replica_groups=mesh['ex'=4,'row'=8,'col'=8] {'ex'}, use_global_device_ids=true, to_apply=%region_6.0 | all-reduce | flops 2432 | bytes 19456 | tf_op jit(solution)/shard_map/psum | solution.py:74
  (56 shorter events, 24.4 us)
Async XLA Ops:
  7.2 254.3 %all-reduce.3.cloned.1.call-start = ((), (), s32[]{:S(2)}) async-start(), calls=%async_computation | async-start | bytes 9437184 | tf_op jit(solution)/shard_map/psum | solution.py:67
  8.1 6.5 %collective-permute-start = (bf16[8,1,32,128]{3,2,1,0:T(8,128)(2,1)S(1)}, bf16[8,1,32,128]{3,2,1,0:T(8,128)(2,1)S(1)}, u32[]{:S(2)}, u32[]{:S(2)}) collective-permute-start(bf16[8,1,32,128]{3,2,1,0:T(8,128)(2,1)S(1)} %get-tuple-element.34), channel_id=1, source_target_pairs={{0,8},{8,16},{16,24},{24,32},{32,40},{40,48},{48,56},{1,9},{9,17},... | collective-permute-start | bytes 196616 | tf_op jit(solution)/shard_map/ppermute | solution.py:17
  12.7 5.6 %collective-permute-start.1 = (bf16[8,1,32,128]{3,2,1,0:T(8,128)(2,1)S(1)}, bf16[8,1,32,128]{3,2,1,0:T(8,128)(2,1)S(1)}, u32[]{:S(2)}, u32[]{:S(2)}) collective-permute-start(bf16[8,1,32,128]{3,2,1,0:T(8,128)(2,1)S(1)} %get-tuple-element.33), channel_id=1, source_target_pairs={{8,0},{16,8},{24,16},{32,24},{40,32},{48,40},{56,48},{9,1},{17,9},... | collective-permute-start | bytes 196616 | tf_op jit(solution)/shard_map/ppermute | solution.py:20
  14.7 12.4 %copy-start.2 = (bf16[3,3,128,128]{3,2,1,0:T(8,128)(2,1)S(1)}, bf16[3,3,128,128]{3,2,1,0:T(8,128)(2,1)}, u32[]{:S(2)}) copy-start(bf16[3,3,128,128]{3,2,1,0:T(8,128)(2,1)} %param.8) | copy-start | bytes 884740
  22.2 5.6 %collective-permute-start.2 = (bf16[8,34,1,128]{3,2,1,0:T(2,128)(2,1)S(1)}, bf16[8,34,1,128]{3,2,1,0:T(2,128)(2,1)S(1)}, u32[]{:S(2)}, u32[]{:S(2)}) collective-permute-start(bf16[8,34,1,128]{3,2,1,0:T(2,128)(2,1)S(1)} %get-tuple-element.24), channel_id=1, source_target_pairs={{0,1},{1,2},{2,3},{3,4},{4,5},{5,6},{6,7},{8,9},{9,10},{10,11},{11... | collective-permute-start | bytes 208904 | tf_op jit(solution)/shard_map/ppermute | solution.py:17
  25.8 6.0 %collective-permute-start.3 = (bf16[8,34,1,128]{3,2,1,0:T(2,128)(2,1)S(1)}, bf16[8,34,1,128]{3,2,1,0:T(2,128)(2,1)S(1)}, u32[]{:S(2)}, u32[]{:S(2)}) collective-permute-start(bf16[8,34,1,128]{3,2,1,0:T(2,128)(2,1)S(1)} %get-tuple-element.25), channel_id=1, source_target_pairs={{1,0},{2,1},{3,2},{4,3},{5,4},{6,5},{7,6},{9,8},{10,9},{11,10},{12... | collective-permute-start | bytes 208904 | tf_op jit(solution)/shard_map/ppermute | solution.py:20
  39.7 0.7 copy-start.4
  41.9 1.6 copy-start
  53.4 1.6 copy-start.1
  180.0 12.3 %collective-permute-start.4 = (bf16[8,1,32,128]{3,2,1,0:T(8,128)(2,1)S(1)}, bf16[8,1,32,128]{3,2,1,0:T(8,128)(2,1)S(1)}, u32[]{:S(2)}, u32[]{:S(2)}) collective-permute-start(bf16[8,1,32,128]{3,2,1,0:T(8,128)(2,1)S(1)} %get-tuple-element.28), channel_id=1, source_target_pairs={{0,8},{8,16},{16,24},{24,32},{32,40},{40,48},{48,56},{1,9},{9,17},... | collective-permute-start | bytes 196616 | tf_op jit(solution)/shard_map/ppermute | solution.py:17
  182.0 11.2 %collective-permute-start.5 = (bf16[8,1,32,128]{3,2,1,0:T(8,128)(2,1)S(1)}, bf16[8,1,32,128]{3,2,1,0:T(8,128)(2,1)S(1)}, u32[]{:S(2)}, u32[]{:S(2)}) collective-permute-start(bf16[8,1,32,128]{3,2,1,0:T(8,128)(2,1)S(1)} %get-tuple-element.29), channel_id=1, source_target_pairs={{8,0},{16,8},{24,16},{32,24},{40,32},{48,40},{56,48},{9,1},{17,9},... | collective-permute-start | bytes 196616 | tf_op jit(solution)/shard_map/ppermute | solution.py:20
  193.4 7.2 %collective-permute-start.6 = (bf16[8,34,1,128]{3,2,1,0:T(2,128)(2,1)S(1)}, bf16[8,34,1,128]{3,2,1,0:T(2,128)(2,1)S(1)}, u32[]{:S(2)}, u32[]{:S(2)}) collective-permute-start(bf16[8,34,1,128]{3,2,1,0:T(2,128)(2,1)S(1)} %get-tuple-element.19), channel_id=1, source_target_pairs={{1,0},{2,1},{3,2},{4,3},{5,4},{6,5},{7,6},{9,8},{10,9},{11,10},{12... | collective-permute-start | bytes 208904 | tf_op jit(solution)/shard_map/ppermute | solution.py:20
  194.7 6.5 %collective-permute-start.7 = (bf16[8,34,1,128]{3,2,1,0:T(2,128)(2,1)S(1)}, bf16[8,34,1,128]{3,2,1,0:T(2,128)(2,1)S(1)}, u32[]{:S(2)}, u32[]{:S(2)}) collective-permute-start(bf16[8,34,1,128]{3,2,1,0:T(2,128)(2,1)S(1)} %get-tuple-element.20), channel_id=1, source_target_pairs={{0,1},{1,2},{2,3},{3,4},{4,5},{5,6},{6,7},{8,9},{9,10},{10,11},{11... | collective-permute-start | bytes 208904 | tf_op jit(solution)/shard_map/ppermute | solution.py:17
  212.3 66.5 %copy-start.3 = (f32[18,128]{1,0:T(8,128)S(1)}, f32[18,128]{1,0:T(8,128)}, u32[]{:S(2)}) copy-start(f32[18,128]{1,0:T(8,128)} %param.10) | copy-start | bytes 27652
  212.3 67.1 %copy-start.5 = (f32[128]{0:T(128)S(1)}, f32[128]{0:T(128)}, u32[]{:S(2)}) copy-start(f32[128]{0:T(128)} %param.11) | copy-start | bytes 1540
Sparse Core Ops, SparseCore 0:
  62.5 198.9 all-reduce.2
where the time goes:
time: 292 us; the launch traced here: 287 us
  blocking collectives  131 us (45%)
  waiting for transfers between devices  59 us (20%)
  starting transfers between devices  28.9 us (10%)
  matrix products  25.2 us (9%)
  other arithmetic  18.6 us (6%)
  between operations  14.4 us (5%)
  local copies, waits for them, and re-layouts  9.99 us (3%)
    psum x1, blocking collectives, local(): summed, bias_sum = lax.psum((partial_value, bias_part), ('row', 'col'))  118 us
    psum x1, waiting for transfers between devices, local(): summed, bias_sum = lax.psum((partial_value, bias_part), ('row', 'col'))  49.2 us
    ppermute x4, starting transfers between devices, with_halo(): lax.ppermute(lax.slice_in_dim(block, 0, width, axis=dim), axis, backward)  14.8 us
    ppermute x4, starting transfers between devices, with_halo(): lax.ppermute(lax.slice_in_dim(block, block.shape[dim] - width, None, axis...  14 us
    psum x1, blocking collectives, local(): total_weight, total_bias = lax.psum((weighted, bias_weighted), 'ex')  13.1 us
    concatenate x4, other arithmetic, with_halo(): block = jnp.concatenate([low, block, high], axis=dim)  12.9 us
    dot_general x9, matrix products, local(): jnp.dot(window, weight[tap_row, tap_col], preferred_element_type=jnp.floa...  10.3 us
    ppermute x4, waiting for transfers between devices, with_halo(): lax.ppermute(lax.slice_in_dim(block, 0, width, axis=dim), axis, backward)  9.23 us
  transfers between devices with their start and end apart: 9, of which 6 were waited for; matrix products, arithmetic and copies ran while one was open for 5% of the time, Pallas kernels for 0%

commit v1 on v0

v1 whole, which is shorter than its diff:
```python
import functools
import math

import jax
import jax.numpy as jnp
from jax import lax
from jax.experimental import pallas as pl
from jax.experimental.pallas import tpu as pltpu
from jax.sharding import PartitionSpec as P

noise_multiplier = 0.002
epsilon = 1e-06
F32 = jnp.float32
BF16 = jnp.bfloat16
N_EX = 8
TILE = 32
CH = 128
PITCH = 48
PIX = TILE * TILE
ROWS = 9 * CH
CHUNK = ROWS // 8
OWN = CHUNK // 8
PIECE = 32


def kernel(
    clip, scale,
    x_hbm, cot_hbm, w_ref, b_ref, nw_ref, nb_ref, xe_ref, xc_ref,
    out_hbm, gw_ref, gb_ref,
    xp, cot, gp, xcol, xcor, gcol, gcor, ge, gc, wide, taps, gt, g32, wback, acc, outb,
    stage, crx, y1own, y1tx, y1rx, y2own, y2tx, y2rx, t32, zst, zrx, zacc, bpart,
    n1st, n1rx, n2st, n2rx, fst, est, erx,
    lx_s, lc_s, lo_s, xh_s, xh_r, gh_s, gh_r, c_s, c_r, y1_s, y1_r, y2_s, y2_r, z_s, z_r,
    n1_s, n1_r, n2_s, n2_r, e_s, e_r,
):
    e, r, c = lax.axis_index("ex"), lax.axis_index("row"), lax.axis_index("col")
    core, y = r % 2, r // 2
    up, down, left, right = (r + 7) % 8, (r + 1) % 8, (c + 7) % 8, (c + 1) % 8
    mate = r + 1 - 2 * core
    flip, mirror = y + 1 - 2 * (y % 2), 3 - y
    p1 = flip + core * (mirror - flip)
    p2 = mirror + core * (flip - mirror)
    far = (y + 2) % 4
    corners = ((up, left), (up, right), (down, left), (down, right))

    def remote(src, dst, s_sem, r_sem, to_row, to_col, to_ex=None):
        return pltpu.make_async_remote_copy(
            src_ref=src, dst_ref=dst, send_sem=s_sem, recv_sem=r_sem,
            device_id=(e if to_ex is None else to_ex, to_row, to_col),
            device_id_type=pl.DeviceIdType.MESH,
        )

    def load_x(n):
        return pltpu.make_async_copy(x_hbm.at[n], xp.at[n, 1 : TILE + 1], lx_s.at[n])

    def load_cot(n):
        return pltpu.make_async_copy(cot_hbm.at[n], cot.at[n], lc_s.at[n])

    for n in range(N_EX):
        load_x(n).start()
    for n in range(N_EX):
        load_cot(n).start()

    barrier = pltpu.get_barrier_semaphore()
    partners = list(corners)
    partners += [((r + k) % 8, c) for k in range(1, 8)]
    partners += [(r, (c + k) % 8) for k in range(1, 8)]
    for to_row, to_col in partners:
        pl.semaphore_signal(barrier, inc=1, device_id=(e, to_row, to_col), device_id_type=pl.DeviceIdType.MESH)
    for k in range(1, 4):
        pl.semaphore_signal(barrier, inc=1, device_id=((e + k) % 4, r, c), device_id_type=pl.DeviceIdType.MESH)

    for a in range(3):
        for b in range(3):
            wback[2 - a, (2 - b) * CH : (3 - b) * CH, :] = w_ref[a, b * CH : (b + 1) * CH, :].T
    t32[...] = jnp.zeros_like(t32)
    pl.semaphore_wait(barrier, 21)

    def x_halo():
        copies = [
            remote(x_hbm.at[:, TILE - 1], xp.at[:, 0], xh_s.at[0], xh_r.at[0], down, c),
            remote(x_hbm.at[:, 0], xp.at[:, TILE + 1], xh_s.at[1], xh_r.at[1], up, c),
            remote(xe_ref.at[1], xcol.at[0], xh_s.at[2], xh_r.at[2], r, right),
            remote(xe_ref.at[0], xcol.at[1], xh_s.at[3], xh_r.at[3], r, left),
        ]
        for k, (to_row, to_col) in enumerate(corners):
            copies.append(
                remote(xc_ref.at[k], xcor.at[3 - k], xh_s.at[4 + k], xh_r.at[7 - k], to_row, to_col)
            )
        return copies

    def g_halo(n):
        copies = [
            remote(gp.at[n, TILE], gp.at[n, 0], gh_s.at[0, n], gh_r.at[0, n], down, c),
            remote(gp.at[n, 1], gp.at[n, TILE + 1], gh_s.at[1, n], gh_r.at[1, n], up, c),
            remote(ge.at[1, n], gcol.at[0, n], gh_s.at[2, n], gh_r.at[2, n], r, right),
            remote(ge.at[0, n], gcol.at[1, n], gh_s.at[3, n], gh_r.at[3, n], r, left),
        ]
        for k, (to_row, to_col) in enumerate(corners):
            copies.append(
                remote(gc.at[k, n], gcor.at[3 - k, n], gh_s.at[4 + k, n], gh_r.at[7 - k, n], to_row, to_col)
            )
        return copies

    def clear(pad, col, cor, n):
        count, at = (N_EX, slice(None)) if n is None else (1, pl.ds(n, 1))
        row_zero = jnp.zeros((count, 1, TILE, CH), BF16)
        col_zero = jnp.zeros((1, count, TILE, CH), BF16)
        cor_zero = jnp.zeros((1, count, 16, CH), BF16)

        @pl.when(r == 0)
        def _():
            pad[at, 0:1] = row_zero
            cor[0:1, at] = cor_zero
            cor[1:2, at] = cor_zero

        @pl.when(r == 7)
        def _():
            pad[at, TILE + 1 : TILE + 2] = row_zero
            cor[2:3, at] = cor_zero
            cor[3:4, at] = cor_zero

        @pl.when(c == 0)
        def _():
            col[0:1, at] = col_zero
            cor[0:1, at] = cor_zero
            cor[2:3, at] = cor_zero

        @pl.when(c == 7)
        def _():
            col[1:2, at] = col_zero
            cor[1:2, at] = cor_zero
            cor[3:4, at] = cor_zero

    def spread(pad, col, cor, n):
        tile = wide.reshape(TILE + 2, PITCH, CH)
        tile[:, 8 : 8 + TILE, :] = pad[n].astype(F32)
        for side, slot in ((0, 7), (1, 8 + TILE)):
            wide[pl.ds(PITCH + slot, TILE, stride=PITCH), :] = col[side, n].astype(F32)
            wide[slot : slot + 1, :] = cor[side, n].astype(F32)[0:1]
            last = (TILE + 1) * PITCH + slot
            wide[last : last + 1, :] = cor[2 + side, n].astype(F32)[0:1]
        taps[:, :, CH : 2 * CH] = pad[n]
        taps[:, :, 0:CH] = tile[:, 7 : 7 + TILE, :].astype(BF16)
        taps[:, :, 2 * CH :] = tile[:, 9 : 9 + TILE, :].astype(BF16)

    def conv(weights):
        total = None
        for a in range(3):
            part = jnp.dot(
                taps[a : a + TILE].reshape(PIX, 3 * CH), weights[a], preferred_element_type=F32
            )
            total = part if total is None else total + part
        return total

    def core_copy(m):
        return remote(stage.at[m, 1 - core], crx.at[m], c_s.at[m], c_r.at[m], mate, c)

    def y1_copy(m):
        return remote(y1tx.at[m], y1rx.at[m], y1_s.at[m], y1_r.at[m], 2 * p1 + core, c)

    def y2_copy(m):
        return remote(y2tx.at[m], y2rx.at[m], y2_s.at[m], y2_r.at[m], 2 * p2 + core, c)

    def z_copy(m, k):
        to = (c + k) % 8
        return remote(zst.at[to, m], zrx.at[c, m], z_s.at[k, m], z_r.at[k, m], r, to)

    def z_arrival(m, k):
        src = (c + 8 - k) % 8
        return remote(zst.at[src, m], zrx.at[src, m], z_s.at[k, m], z_r.at[k, m], r, src)

    def step_y1(m):
        core_copy(m).wait_recv()

        def both(j):
            return stage[m, core, j].astype(F32) + crx[m, j].astype(F32)

        y1tx[m, 0] = both(p1).astype(BF16)
        y1tx[m, 1] = both(far).astype(BF16)
        y1_copy(m).start()
        y1own[m, 0] = both(y)
        y1own[m, 1] = both(p2)

    def step_y2(m):
        y1_copy(m).wait_recv()
        y2tx[m] = (y1own[m, 1] + y1rx[m, 1].astype(F32)).astype(BF16)
        y2_copy(m).start()
        y2own[m] = y1own[m, 0] + y1rx[m, 0].astype(F32)

    def step_z(m):
        y2_copy(m).wait_recv()
        t32[0:CHUNK, :] = y2own[m] + y2rx[m].astype(F32)
        for k in range(8):
            piece = t32[k * OWN : k * OWN + PIECE, :].astype(BF16)
            zst[k, m] = piece
        for k in range(1, 8):
            z_copy(m, k).start()
        zrx[c, m] = zst[c, m]

    for copy in x_halo():
        copy.start()
    for copy in x_halo():
        copy.wait_recv()
    for n in range(N_EX):
        load_x(n).wait()
    clear(xp, xcol, xcor, None)

    def first(n, carry):
        spread(xp, xcol, xcor, n)
        load_cot(n).wait()
        acc[...] = conv(w_ref)
        z = acc[...] + b_ref[...]
        s = 1.0 / (1.0 + jnp.exp(-z))
        slope = s * (1.0 + z * (1.0 - s))
        g = (cot[n].reshape(PIX, CH).astype(F32) * slope).astype(BF16)
        gp[n, 1 : TILE + 1] = g.reshape(TILE, TILE, CH)
        wide_g = g.astype(F32)
        g32[...] = wide_g
        bpart[n] = jnp.sum(wide_g.reshape(PIX // 8, 8, CH), axis=0)
        ge[0, n] = g32[pl.ds(0, TILE, stride=TILE), :].astype(BF16)
        ge[1, n] = g32[pl.ds(TILE - 1, TILE, stride=TILE), :].astype(BF16)
        for k, at in enumerate((0, TILE - 1, PIX - TILE, PIX - 1)):
            gc[k, n] = jnp.broadcast_to(g32[at : at + 1, :], (16, CH)).astype(BF16)
        for copy in g_halo(n):
            copy.start()
        gt[...] = gp[n, 1 : TILE + 1].reshape(PIX, CH).T
        for a in range(3):
            part = jnp.dot(
                gt[...], taps[a : a + TILE].reshape(PIX, 3 * CH), preferred_element_type=F32
            )
            for b in range(3):
                block = part[:, b * CH : (b + 1) * CH].T.astype(BF16)
                for k in range(8):
                    group = (3 * a + b) * 8 + k
                    owner, at = group // 9, group % 9 * 16
                    stage[n, owner % 2, owner // 2, at : at + 16, :] = block[16 * k : 16 * k + 16]
        core_copy(n).start()

        @pl.when(n >= 1)
        def _():
            step_y1(n - 1)

        @pl.when(n >= 3)
        def _():
            step_y2(n - 3)

        @pl.when(n >= 5)
        def _():
            step_z(n - 5)

        return carry

    lax.fori_loop(0, N_EX, first, 0)

    def store_out(n):
        return pltpu.make_async_copy(outb.at[n], out_hbm.at[n], lo_s.at[n])

    plan = {
        0: ((step_z, 3), (step_y2, 5)),
        1: ((step_y1, 7),),
        2: ((step_z, 4), (step_y2, 6)),
        3: ((step_z, 5),),
        5: ((step_z, 6), (step_y2, 7)),
        7: ((step_z, 7),),
    }

    def second(n, carry):
        for copy in g_halo(n):
            copy.wait_recv()
        clear(gp, gcol, gcor, n)
        spread(gp, gcol, gcor, n)
        outb[n] = conv(wback).astype(BF16).reshape(TILE, TILE, CH)
        store_out(n).start()
        for when, steps in plan.items():

            @pl.when(n == when)
            def _(steps=steps):
                for step, m in steps:
                    step(m)

        return carry

    lax.fori_loop(0, N_EX, second, 0)

    keep = lax.broadcasted_iota(jnp.int32, (8, CH), 0) < OWN - 16
    for m in range(N_EX):
        for k in range(1, 8):
            z_arrival(m, k).wait_recv()
        total = zrx[0, m].astype(F32)
        for k in range(1, 8):
            total = total + zrx[k, m].astype(F32)
        zacc[m] = total[0:24]
        square = total * total
        part = square[0:8] + square[8:16] + jnp.where(keep, square[16:24], 0.0)
        n1st[m : m + 1, :] = jnp.sum(part, axis=0, keepdims=True)
        n1st[N_EX + m : N_EX + m + 1, :] = jnp.sum(bpart[m], axis=0, keepdims=True)

    def n1_copy(k):
        return remote(n1st, n1rx.at[c], n1_s.at[k], n1_r.at[k], r, (c + k) % 8)

    def n1_arrival(k):
        return remote(n1st, n1rx.at[(c + 8 - k) % 8], n1_s.at[k], n1_r.at[k], r, (c + 8 - k) % 8)

    def n2_copy(k):
        return remote(n2st, n2rx.at[r], n2_s.at[k], n2_r.at[k], (r + k) % 8, c)

    def n2_arrival(k):
        return remote(n2st, n2rx.at[(r + 8 - k) % 8], n2_s.at[k], n2_r.at[k], (r + 8 - k) % 8, c)

    def e_copy(k):
        return remote(est, erx.at[e], e_s.at[k], e_r.at[k], r, c, (e + k) % 4)

    def e_arrival(k):
        return remote(est, erx.at[(e + 4 - k) % 4], e_s.at[k], e_r.at[k], r, c, (e + 4 - k) % 4)

    for k in (4, 3, 5, 2, 6, 1, 7):
        n1_copy(k).start()
    n1rx[c] = n1st[...]
    for k in range(1, 8):
        n1_arrival(k).wait_recv()
    total = n1rx[0]
    for k in range(1, 8):
        total = total + n1rx[k]
    n2st[...] = total
    for k in (4, 3, 5, 2, 6, 1, 7):
        n2_copy(k).start()
    n2rx[r] = total
    for k in range(1, 8):
        n2_arrival(k).wait_recv()
    total = n2rx[0]
    for k in range(1, 8):
        total = total + n2rx[k]
    bias_sum = total[N_EX:]
    squares = jnp.sum(total[0:N_EX] + bias_sum * bias_sum, axis=1, keepdims=True)
    factor = jnp.minimum(1.0, clip / jnp.sqrt(squares + epsilon))
    fst[...] = jnp.broadcast_to(factor, (N_EX, CH))
    weighted = fst[0:1, :] * zacc[0]
    for m in range(1, N_EX):
        weighted = weighted + fst[m : m + 1, :] * zacc[m]
    est[...] = weighted
    est[OWN : OWN + 1, :] = jnp.sum(fst[...] * bias_sum, axis=0, keepdims=True)
    for k in (2, 1, 3):
        e_copy(k).start()
    erx[e] = est[...]
    for k in range(1, 4):
        e_arrival(k).wait_recv()
    total = (erx[0] + erx[1]) + (erx[2] + erx[3])
    gw_ref[...] = (total[0:OWN] + noise_multiplier * clip * nw_ref[...]) * scale
    gb_ref[...] = (total[OWN : OWN + 1] + noise_multiplier * clip * nb_ref[...]) * scale

    for copy in x_halo():
        copy.wait_send()

    def drain(n, carry):
        for copy in g_halo(n):
            copy.wait_send()
        core_copy(n).wait_send()
        y1_copy(n).wait_send()
        y2_copy(n).wait_send()
        for k in range(1, 8):
            z_copy(n, k).wait_send()
        store_out(n).wait()
        return carry

    lax.fori_loop(0, N_EX, drain, 0)
    for k in range(1, 8):
        n1_copy(k).wait_send()
        n2_copy(k).wait_send()
    for k in range(1, 4):
        e_copy(k).wait_send()


def local(inputs, cotangent, weight, bias, noise_weight, noise_bias):
    examples, tile_rows, tile_cols, channels = inputs.shape
    height = tile_rows * lax.axis_size("row")
    width = tile_cols * lax.axis_size("col")
    clip = math.sqrt(height * width * 9 * channels * channels)
    scale = 1.0 / math.sqrt(examples * lax.axis_size("ex") * height * width)
    edges = jnp.stack([inputs[:, :, 0], inputs[:, :, -1]])
    spots = jnp.stack([inputs[:, i, j] for i in (0, -1) for j in (0, -1)])
    spots = jnp.broadcast_to(spots[:, :, None], (4, examples, 16, channels))
    vmem, anywhere = pl.BlockSpec(memory_space=pltpu.VMEM), pl.BlockSpec(memory_space=pl.ANY)
    halo_col, halo_cor = pltpu.VMEM((2, N_EX, TILE, CH), BF16), pltpu.VMEM((4, N_EX, 16, CH), BF16)
    dma = pltpu.SemaphoreType.DMA
    input_grad, grad_weight, grad_bias = pl.pallas_call(
        functools.partial(kernel, clip, scale),
        out_shape=(
            jax.ShapeDtypeStruct(inputs.shape, BF16),
            jax.ShapeDtypeStruct(noise_weight.shape, F32),
            jax.ShapeDtypeStruct((1, channels), F32),
        ),
        in_specs=[anywhere, anywhere] + [vmem] * 6,
        out_specs=[anywhere, vmem, vmem],
        scratch_shapes=[
            pltpu.VMEM((N_EX, TILE + 2, TILE, CH), BF16),
            pltpu.VMEM((N_EX, TILE, TILE, CH), BF16),
            pltpu.VMEM((N_EX, TILE + 2, TILE, CH), BF16),
            halo_col, halo_cor, halo_col, halo_cor, halo_col, halo_cor,
            pltpu.VMEM(((TILE + 2) * PITCH, CH), F32),
            pltpu.VMEM((TILE + 2, TILE, 3 * CH), BF16),
            pltpu.VMEM((CH, PIX), BF16),
            pltpu.VMEM((PIX, CH), F32),
            pltpu.VMEM((3, 3 * CH, CH), BF16),
            pltpu.VMEM((PIX, CH), F32),
            pltpu.VMEM((N_EX, TILE, TILE, CH), BF16),
            pltpu.VMEM((N_EX, 2, 4, CHUNK, CH), BF16),
            pltpu.VMEM((N_EX, 4, CHUNK, CH), BF16),
            pltpu.VMEM((N_EX, 2, CHUNK, CH), F32),
            pltpu.VMEM((N_EX, 2, CHUNK, CH), BF16),
            pltpu.VMEM((N_EX, 2, CHUNK, CH), BF16),
            pltpu.VMEM((N_EX, CHUNK, CH), F32),
            pltpu.VMEM((N_EX, CHUNK, CH), BF16),
            pltpu.VMEM((N_EX, CHUNK, CH), BF16),
            pltpu.VMEM((CHUNK + 16, CH), F32),
            pltpu.VMEM((8, N_EX, PIECE, CH), BF16),
            pltpu.VMEM((8, N_EX, PIECE, CH), BF16),
            pltpu.VMEM((N_EX, 24, CH), F32),
            pltpu.VMEM((N_EX, 8, CH), F32),
            pltpu.VMEM((2 * N_EX, CH), F32),
            pltpu.VMEM((8, 2 * N_EX, CH), F32),
            pltpu.VMEM((2 * N_EX, CH), F32),
            pltpu.VMEM((8, 2 * N_EX, CH), F32),
            pltpu.VMEM((N_EX, CH), F32),
            pltpu.VMEM((24, CH), F32),
            pltpu.VMEM((4, 24, CH), F32),
            dma((N_EX,)), dma((N_EX,)), dma((N_EX,)),
            dma((8,)), dma((8,)), dma((8, N_EX)), dma((8, N_EX)),
            dma((N_EX,)), dma((N_EX,)), dma((N_EX,)), dma((N_EX,)), dma((N_EX,)), dma((N_EX,)),
            dma((8, N_EX)), dma((8, N_EX)),
            dma((8,)), dma((8,)), dma((8,)), dma((8,)), dma((4,)), dma((4,)),
        ],
        compiler_params=pltpu.CompilerParams(
            collective_id=0, has_side_effects=True, vmem_limit_bytes=48 * 2**20
        ),
        name="clipped_grad",
    )(
        inputs, cotangent, weight.reshape(3, 3 * channels, channels), bias.reshape(1, channels),
        noise_weight, noise_bias.reshape(1, channels), edges, spots,
    )
    return input_grad, grad_weight, grad_bias.reshape(channels)


def solution(mesh):
    in_specs = (
        P("ex", "row", "col", None),
        P("ex", "row", "col", None),
        P(),
        P(),
        P(("row", "col"), None),
        P(),
    )
    out_specs = (P("ex", "row", "col", None), P(("row", "col"), None), P())
    return jax.shard_map(local, mesh=mesh, in_specs=in_specs, out_specs=out_specs, check_vma=False)
```

time: 292 us -> 71.1 us (0.24); the launches traced: 287 us -> 70.8 us
  blocking collectives: 131 us -> 0 us
  Pallas kernels: 0 us -> 60.8 us
  waiting for transfers between devices: 59 us -> 0 us
  starting transfers between devices: 28.9 us -> 0 us
  matrix products: 25.2 us -> 0 us
  other arithmetic: 18.6 us -> 0.03 us
  between operations: 14.4 us -> 0.71 us
    psum x2 -> x0, blocking collectives: 131 us -> none  [the longest x1 118 us: local(): summed, bias_sum = lax.psum((partial_value, bias_part), ('row', 'col'))]
    pallas_call x0 -> x1, Pallas kernels: none -> 60.8 us  [local(): pl.pallas_call(functools.partial(kernel, clip, scale), out_shape=(jax.Sha...]
    psum x1 -> x0, waiting for transfers between devices: 49.2 us -> none  [local(): summed, bias_sum = lax.psum((partial_value, bias_part), ('row', 'col'))]
    ppermute x8 -> x0, starting transfers between devices: 28.8 us -> none  [the longest x4 14.8 us: with_halo(): lax.ppermute(lax.slice_in_dim(block, 0, width, axis=dim), axis, backward)]
    dot_general x27 -> x0, matrix products: 25.2 us -> none  [the longest x9 10.3 us: local(): jnp.dot(window, weight[tap_row, tap_col], preferred_element_type=jnp.floa...]
    concatenate x4 -> x0, other arithmetic: 12.9 us -> none  [with_halo(): block = jnp.concatenate([low, block, high], axis=dim)]
    ppermute x8 -> x0, waiting for transfers between devices: 9.83 us -> none  [the longest x4 9.23 us: with_halo(): lax.ppermute(lax.slice_in_dim(block, 0, width, axis=dim), axis, backward)]
    unnamed x13, local copies, waits for them, and re-layouts: 1.73 us -> 6.99 us
  transfers between devices with their start and end apart: 9 -> 0, of which waited for: 6 -> 0; matrix products, arithmetic and copies ran while one was open for 5% -> 0% of each run, Pallas kernels for 0% -> 0%
where the time goes in v1:
time: 71.1 us; the launch traced here: 70.8 us
  Pallas kernels  60.8 us (86%)
  local copies, waits for them, and re-layouts  9.3 us (13%)
    pallas_call x1, Pallas kernels, local(): pl.pallas_call(functools.partial(kernel, clip, scale), out_shape=(jax.Sha...  60.8 us
    unnamed x13, local copies, waits for them, and re-layouts  6.99 us
    slice x1, local copies, waits for them, and re-layouts, local(): edges = jnp.stack([inputs[:, :, 0], inputs[:, :, -1]])  1.47 us

profile of v1, /device:TPU:1, one launch (start us, length us, event | category | flops | bytes accessed | tf_op | source)
XLA Modules:
  0.0 70.8 jit_solution(5353098303996362284)
XLA Ops:
  0.6 0.8 %fusion = (bf16[8,1,1,128]{3,2,1,0:T(2,128)(2,1)S(1)}, bf16[8,1,1,128]{3,2,1,0:T(2,128)(2,1)S(1)}, bf16[8,1,1,128]{3,2,1,0:T(2,128)(2,1)S(1)}, bf16[8,1,1,128]{3,2,1,0:T(2,128)(2,1)S(1)}) fusion(bf16[8,32,32,128]{3,2,1,0:T(8,128)(2,1)} %x_hbm.1), kind=kLoop, calls=%fused_computation.8 | loop fusion | bytes 16384 | tf_op jit(solution)/shard_map/slice | solution.py:381
  1.5 1.5 %fusion.1 = (bf16[8,32,1,128]{3,2,1,0:T(2,128)(2,1)S(1)}, bf16[8,32,1,128]{3,2,1,0:T(2,128)(2,1)S(1)}) fusion(bf16[8,32,32,128]{3,2,1,0:T(8,128)(2,1)} %x_hbm.1), kind=kLoop, calls=%fused_computation.9 | loop fusion | bytes 262144 | tf_op jit(solution)/shard_map/slice | solution.py:380
  3.0 0.0 copy-start
  3.0 1.6 %copy-done = bf16[8,32,32,128]{3,2,1,0:T(8,128)(2,1)S(1)} copy-done((bf16[8,32,32,128]{3,2,1,0:T(8,128)(2,1)S(1)}, bf16[8,32,32,128]{3,2,1,0:T(8,128)(2,1)}, u32[]{:S(2)}) %copy-start) | copy-done | bytes 2097176
  4.6 0.0 copy-start.1
  4.6 1.0 %copy-done.1 = bf16[3,3,128,128]{3,2,1,0:T(8,128)(2,1)S(1)} copy-done((bf16[3,3,128,128]{3,2,1,0:T(8,128)(2,1)S(1)}, bf16[3,3,128,128]{3,2,1,0:T(8,128)(2,1)}, u32[]{:S(2)}) %copy-start.1) | copy-done | bytes 294936
  5.6 0.0 copy-start.2
  5.6 0.7 copy-done.2
  6.3 0.0 copy-start.3
  6.3 0.7 copy-done.3
  6.9 0.0 copy-start.4
  6.9 0.7 copy-done.4
  7.6 60.8 %clipped_grad.1 = (bf16[8,32,32,128]{3,2,1,0:T(8,128)(2,1)S(1)}, f32[18,128]{1,0:T(8,128)S(1)}, f32[1,128]{1,0:T(1,128)S(1)}) custom-call(bf16[8,32,32,128]{3,2,1,0:T(8,128)(2,1)S(1)} %copy-done, bf16[8,32,32,128]{3,2,1,0:T(8,128)(2,1)} %cot_hbm.1, bf16[3,384,128]{2,1,0:T(8,128)(2,1)S(1)} %bitcast.16, f32[1,128]{1,0:T(1,128)S(1)} %bitcast.17, ...), custom_call_target="tpu_custom_call" | custom-call | tf_op jit(solution)/shard_map/clipped_grad/pallas_call | solution.py:386
  68.4 1.3 %copy.35 = bf16[8,32,32,128]{3,2,1,0:T(8,128)(2,1)} copy(bf16[8,32,32,128]{3,2,1,0:T(8,128)(2,1)S(1)} %get-tuple-element.24) | data formatting | bytes 4194304
  69.7 0.6 copy.36
  70.3 0.5 copy.37
  (6 shorter events, 0.1 us)
Async XLA Ops:
  3.0 1.6 %copy-start = (bf16[8,32,32,128]{3,2,1,0:T(8,128)(2,1)S(1)}, bf16[8,32,32,128]{3,2,1,0:T(8,128)(2,1)}, u32[]{:S(2)}) copy-start(bf16[8,32,32,128]{3,2,1,0:T(8,128)(2,1)} %x_hbm.1) | copy-start | bytes 6291460
  4.6 1.0 %copy-start.1 = (bf16[3,3,128,128]{3,2,1,0:T(8,128)(2,1)S(1)}, bf16[3,3,128,128]{3,2,1,0:T(8,128)(2,1)}, u32[]{:S(2)}) copy-start(bf16[3,3,128,128]{3,2,1,0:T(8,128)(2,1)} %param.8) | copy-start | bytes 884740
  5.6 0.7 copy-start.2
  6.3 0.7 copy-start.3
  6.9 0.7 copy-start.4

commit v2 on v1

--- a/solution.py
+++ b/solution.py
@@ -24,13 +24,13 @@
 
 
 def kernel(
-    clip, scale,
-    x_hbm, cot_hbm, w_ref, b_ref, nw_ref, nb_ref, xe_ref, xc_ref,
-    out_hbm, gw_ref, gb_ref,
-    xp, cot, gp, xcol, xcor, gcol, gcor, ge, gc, wide, taps, gt, g32, wback, acc, outb,
+    clip,
+    x_hbm, cot_hbm, w_hbm, b_hbm,
+    out_hbm, sum_ref,
+    w_ref, b_ref, xe_ref, xc_ref, edge, xp, cot, gp, xcol, xcor, gcol, gcor, ge, gc, wide, taps, gt, g32, wback, acc, outb,
     stage, crx, y1own, y1tx, y1rx, y2own, y2tx, y2rx, t32, zst, zrx, zacc, bpart,
     n1st, n1rx, n2st, n2rx, fst, est, erx,
-    lx_s, lc_s, lo_s, xh_s, xh_r, gh_s, gh_r, c_s, c_r, y1_s, y1_r, y2_s, y2_r, z_s, z_r,
+    lw_s, lx_s, lc_s, lo_s, xh_s, xh_r, gh_s, gh_r, c_s, c_r, y1_s, y1_r, y2_s, y2_r, z_s, z_r,
     n1_s, n1_r, n2_s, n2_r, e_s, e_r,
 ):
     e, r, c = lax.axis_index("ex"), lax.axis_index("row"), lax.axis_index("col")
@@ -56,8 +56,12 @@
     def load_cot(n):
         return pltpu.make_async_copy(cot_hbm.at[n], cot.at[n], lc_s.at[n])
 
+    load_w = pltpu.make_async_copy(w_hbm, w_ref, lw_s.at[0])
+    load_b = pltpu.make_async_copy(b_hbm, b_ref, lw_s.at[1])
     for n in range(N_EX):
         load_x(n).start()
+    load_w.start()
+    load_b.start()
     for n in range(N_EX):
         load_cot(n).start()
 
@@ -70,6 +74,20 @@
     for k in range(1, 4):
         pl.semaphore_signal(barrier, inc=1, device_id=((e + k) % 4, r, c), device_id_type=pl.DeviceIdType.MESH)
 
+    def take_edges(n, carry):
+        load_x(n).wait()
+        for side in range(2):
+            block = xp[n, 1 : TILE + 1, side * 16 : side * 16 + 16, :].astype(F32)
+            edge[...] = block.reshape(TILE * 16, CH)
+            column = edge[pl.ds(15 * side, TILE, stride=16), :]
+            xe_ref[side, n] = column.astype(BF16)
+            xc_ref[side, n] = jnp.broadcast_to(column[0:1], (16, CH)).astype(BF16)
+            xc_ref[2 + side, n] = jnp.broadcast_to(column[TILE - 1 : TILE], (16, CH)).astype(BF16)
+        return carry
+
+    lax.fori_loop(0, N_EX, take_edges, 0)
+    load_w.wait()
+    load_b.wait()
     for a in range(3):
         for b in range(3):
             wback[2 - a, (2 - b) * CH : (3 - b) * CH, :] = w_ref[a, b * CH : (b + 1) * CH, :].T
@@ -202,8 +220,6 @@
         copy.start()
     for copy in x_halo():
         copy.wait_recv()
-    for n in range(N_EX):
-        load_x(n).wait()
     clear(xp, xcol, xcor, None)
 
     def first(n, carry):
@@ -345,9 +361,7 @@
     erx[e] = est[...]
     for k in range(1, 4):
         e_arrival(k).wait_recv()
-    total = (erx[0] + erx[1]) + (erx[2] + erx[3])
-    gw_ref[...] = (total[0:OWN] + noise_multiplier * clip * nw_ref[...]) * scale
-    gb_ref[...] = (total[OWN : OWN + 1] + noise_multiplier * clip * nb_ref[...]) * scale
+    sum_ref[...] = (erx[0] + erx[1]) + (erx[2] + erx[3])
 
     for copy in x_halo():
         copy.wait_send()
@@ -377,22 +391,22 @@
     width = tile_cols * lax.axis_size("col")
     clip = math.sqrt(height * width * 9 * channels * channels)
     scale = 1.0 / math.sqrt(examples * lax.axis_size("ex") * height * width)
-    edges = jnp.stack([inputs[:, :, 0], inputs[:, :, -1]])
-    spots = jnp.stack([inputs[:, i, j] for i in (0, -1) for j in (0, -1)])
-    spots = jnp.broadcast_to(spots[:, :, None], (4, examples, 16, channels))
     vmem, anywhere = pl.BlockSpec(memory_space=pltpu.VMEM), pl.BlockSpec(memory_space=pl.ANY)
     halo_col, halo_cor = pltpu.VMEM((2, N_EX, TILE, CH), BF16), pltpu.VMEM((4, N_EX, 16, CH), BF16)
     dma = pltpu.SemaphoreType.DMA
-    input_grad, grad_weight, grad_bias = pl.pallas_call(
-        functools.partial(kernel, clip, scale),
+    input_grad, total = pl.pallas_call(
+        functools.partial(kernel, clip),
         out_shape=(
             jax.ShapeDtypeStruct(inputs.shape, BF16),
-            jax.ShapeDtypeStruct(noise_weight.shape, F32),
-            jax.ShapeDtypeStruct((1, channels), F32),
+            jax.ShapeDtypeStruct((24, channels), F32),
         ),
-        in_specs=[anywhere, anywhere] + [vmem] * 6,
-        out_specs=[anywhere, vmem, vmem],
+        in_specs=[pl.BlockSpec(memory_space=pltpu.MemorySpace.HBM)] * 4,
+        out_specs=[anywhere, vmem],
         scratch_shapes=[
+            pltpu.VMEM((3, 3 * CH, CH), BF16),
+            pltpu.VMEM((1, CH), F32),
+            halo_col, halo_cor,
+            pltpu.VMEM((TILE * 16, CH), F32),
             pltpu.VMEM((N_EX, TILE + 2, TILE, CH), BF16),
             pltpu.VMEM((N_EX, TILE, TILE, CH), BF16),
             pltpu.VMEM((N_EX, TILE + 2, TILE, CH), BF16),
@@ -424,21 +438,22 @@
             pltpu.VMEM((N_EX, CH), F32),
             pltpu.VMEM((24, CH), F32),
             pltpu.VMEM((4, 24, CH), F32),
-            dma((N_EX,)), dma((N_EX,)), dma((N_EX,)),
+            dma((2,)), dma((N_EX,)), dma((N_EX,)), dma((N_EX,)),
             dma((8,)), dma((8,)), dma((8, N_EX)), dma((8, N_EX)),
             dma((N_EX,)), dma((N_EX,)), dma((N_EX,)), dma((N_EX,)), dma((N_EX,)), dma((N_EX,)),
             dma((8, N_EX)), dma((8, N_EX)),
             dma((8,)), dma((8,)), dma((8,)), dma((8,)), dma((4,)), dma((4,)),
         ],
         compiler_params=pltpu.CompilerParams(
-            collective_id=0, has_side_effects=True, vmem_limit_bytes=48 * 2**20
+            collective_id=0, has_side_effects=True
         ),
         name="clipped_grad",
     )(
-        inputs, cotangent, weight.reshape(3, 3 * channels, channels), bias.reshape(1, channels),
-        noise_weight, noise_bias.reshape(1, channels), edges, spots,
+        inputs, cotangent, weight.reshape(3, 3 * channels, channels), bias.reshape(1, channels)
     )
-    return input_grad, grad_weight, grad_bias.reshape(channels)
+    grad_weight = (total[0:OWN] + noise_multiplier * clip * noise_weight) * scale
+    grad_bias = (total[OWN] + noise_multiplier * clip * noise_bias) * scale
+    return input_grad, grad_weight, grad_bias
 
 
 def solution(mesh):

time: 71.1 us -> 68.4 us (0.962)
  local copies, waits for them, and re-layouts: 9.3 us -> 3.28 us
  other arithmetic: 0.03 us -> 2.51 us
  Pallas kernels: 60.8 us -> 61.8 us
    unnamed x13 -> x5, local copies, waits for them, and re-layouts: 6.99 us -> 3.28 us
    mul x0 -> x2, other arithmetic: none -> 2.51 us  [the longest x1 1.31 us: local(): (total[0:OWN] + noise_multiplier * clip * noise_weight) * scale]
    slice x2 -> x0, local copies, waits for them, and re-layouts: 2.26 us -> none  [the longest x1 1.47 us: local(): edges = jnp.stack([inputs[:, :, 0], inputs[:, :, -1]])]
    pallas_call x1, Pallas kernels: 60.8 us -> 61.8 us  [local(): pl.pallas_call(functools.partial(kernel, clip), out_shape=(jax.ShapeDtype...]
where the time goes in v2:
time: 68.4 us; the launch traced here: 68.2 us
  Pallas kernels  61.8 us (90%)
  local copies, waits for them, and re-layouts  3.28 us (5%)
  other arithmetic  2.51 us (4%)
    pallas_call x1, Pallas kernels, local(): pl.pallas_call(functools.partial(kernel, clip), out_shape=(jax.ShapeDtype...  61.8 us
    unnamed x5, local copies, waits for them, and re-layouts  3.28 us

profile of v2, /device:TPU:1, one launch (start us, length us, event | category | flops | bytes accessed | tf_op | source)
XLA Modules:
  0.0 68.2 jit_solution(15042106080629516757)
XLA Ops:
  0.6 0.0 copy-start.1
  0.6 0.0 copy-start
  0.7 61.8 %clipped_grad.1 = (bf16[8,32,32,128]{3,2,1,0:T(8,128)(2,1)}, f32[24,128]{1,0:T(8,128)}) custom-call(bf16[8,32,32,128]{3,2,1,0:T(8,128)(2,1)} %x_hbm.1, bf16[8,32,32,128]{3,2,1,0:T(8,128)(2,1)} %cot_hbm.1, bf16[3,384,128]{2,1,0:T(8,128)(2,1)} %bitcast.6, f32[1,128]{1,0:T(1,128)} %bitcast.7), custom_call_target="tpu_custom_call" | custom-call | tf_op jit(solution)/shard_map/clipped_grad/pallas_call | solution.py:397
  62.4 0.0 copy-done.1
  62.4 1.2 %fusion = f32[128]{0:T(128)} fusion(f32[128]{0:T(128)S(1)} %copy-done.1, f32[24,128]{1,0:T(8,128)} %get-tuple-element.6), kind=kLoop, calls=%fused_computation.2 | loop fusion | flops 384 | bytes 1536 | tf_op jit(solution)/shard_map/mul | solution.py:455
  63.6 0.0 copy-done
  63.6 1.3 %add_multiply_fusion = f32[18,128]{1,0:T(8,128)} fusion(f32[18,128]{1,0:T(8,128)S(1)} %copy-done, f32[24,128]{1,0:T(8,128)} %get-tuple-element.6), kind=kLoop, calls=%fused_computation | loop fusion | flops 6912 | bytes 27648 | tf_op jit(solution)/shard_map/mul | solution.py:454
  64.9 3.3 %copy.10 = bf16[8,32,32,128]{3,2,1,0:T(8,128)(2,1)} copy(bf16[8,32,32,128]{3,2,1,0:T(8,128)(2,1)} %get-tuple-element.10) | data formatting | bytes 4194304
Async XLA Ops:
  0.6 61.8 %copy-start.1 = (f32[128]{0:T(128)S(1)}, f32[128]{0:T(128)}, u32[]{:S(2)}) copy-start(f32[128]{0:T(128)} %param.11) | copy-start | bytes 1540
  0.6 63.0 %copy-start = (f32[18,128]{1,0:T(8,128)S(1)}, f32[18,128]{1,0:T(8,128)}, u32[]{:S(2)}) copy-start(f32[18,128]{1,0:T(8,128)} %param.10) | copy-start | bytes 27652

commit v3 on v2

--- a/solution.py
+++ b/solution.py
@@ -29,9 +29,9 @@
     out_hbm, sum_ref,
     w_ref, b_ref, xe_ref, xc_ref, edge, xp, cot, gp, xcol, xcor, gcol, gcor, ge, gc, wide, taps, gt, g32, wback, acc, outb,
     stage, crx, y1own, y1tx, y1rx, y2own, y2tx, y2rx, t32, zst, zrx, zacc, bpart,
-    n1st, n1rx, n2st, n2rx, fst, est, erx,
+    b1st, b1rx, b2st, b2rx, n1st, n1rx, n2st, n2rx, fst, est, erx,
     lw_s, lx_s, lc_s, lo_s, xh_s, xh_r, gh_s, gh_r, c_s, c_r, y1_s, y1_r, y2_s, y2_r, z_s, z_r,
-    n1_s, n1_r, n2_s, n2_r, e_s, e_r,
+    b1_s, b1_r, b2_s, b2_r, n1_s, n1_r, n2_s, n2_r, e_s, e_r,
 ):
     e, r, c = lax.axis_index("ex"), lax.axis_index("row"), lax.axis_index("col")
     core, y = r % 2, r // 2
@@ -50,11 +50,14 @@
             device_id_type=pl.DeviceIdType.MESH,
         )
 
+    def received(view, sem):
+        remote(view, view, sem, sem, r, c).wait_recv()
+
+    def sent(view, sem):
+        remote(view, view, sem, sem, r, c).wait_send()
+
     def load_x(n):
         return pltpu.make_async_copy(x_hbm.at[n], xp.at[n, 1 : TILE + 1], lx_s.at[n])
-
-    def load_cot(n):
-        return pltpu.make_async_copy(cot_hbm.at[n], cot.at[n], lc_s.at[n])
 
     load_w = pltpu.make_async_copy(w_hbm, w_ref, lw_s.at[0])
     load_b = pltpu.make_async_copy(b_hbm, b_ref, lw_s.at[1])
@@ -62,8 +65,8 @@
         load_x(n).start()
     load_w.start()
     load_b.start()
-    for n in range(N_EX):
-        load_cot(n).start()
+    load_cot = pltpu.make_async_copy(cot_hbm, cot, lc_s)
+    load_cot.start()
 
     barrier = pltpu.get_barrier_semaphore()
     partners = list(corners)
@@ -81,8 +84,8 @@
             edge[...] = block.reshape(TILE * 16, CH)
             column = edge[pl.ds(15 * side, TILE, stride=16), :]
             xe_ref[side, n] = column.astype(BF16)
-            xc_ref[side, n] = jnp.broadcast_to(column[0:1], (16, CH)).astype(BF16)
-            xc_ref[2 + side, n] = jnp.broadcast_to(column[TILE - 1 : TILE], (16, CH)).astype(BF16)
+            xc_ref[side, pl.ds(n, 1), :] = column[0:1]
+            xc_ref[2 + side, pl.ds(n, 1), :] = column[TILE - 1 : TILE]
         return carry
 
     lax.fori_loop(0, N_EX, take_edges, 0)
@@ -96,35 +99,33 @@
 
     def x_halo():
         copies = [
-            remote(x_hbm.at[:, TILE - 1], xp.at[:, 0], xh_s.at[0], xh_r.at[0], down, c),
-            remote(x_hbm.at[:, 0], xp.at[:, TILE + 1], xh_s.at[1], xh_r.at[1], up, c),
-            remote(xe_ref.at[1], xcol.at[0], xh_s.at[2], xh_r.at[2], r, right),
-            remote(xe_ref.at[0], xcol.at[1], xh_s.at[3], xh_r.at[3], r, left),
+            remote(x_hbm.at[:, TILE - 1], xp.at[:, 0], xh_s, xh_r, down, c),
+            remote(x_hbm.at[:, 0], xp.at[:, TILE + 1], xh_s, xh_r, up, c),
+            remote(xe_ref.at[1], xcol.at[0], xh_s, xh_r, r, right),
+            remote(xe_ref.at[0], xcol.at[1], xh_s, xh_r, r, left),
         ]
         for k, (to_row, to_col) in enumerate(corners):
-            copies.append(
-                remote(xc_ref.at[k], xcor.at[3 - k], xh_s.at[4 + k], xh_r.at[7 - k], to_row, to_col)
-            )
+            copies.append(remote(xc_ref.at[k], xcor.at[3 - k], xh_s, xh_r, to_row, to_col))
         return copies
+
+    x_bytes = acc.at[0 : 4 * N_EX * TILE // 2 + 4 * N_EX]
 
     def g_halo(n):
         copies = [
-            remote(gp.at[n, TILE], gp.at[n, 0], gh_s.at[0, n], gh_r.at[0, n], down, c),
-            remote(gp.at[n, 1], gp.at[n, TILE + 1], gh_s.at[1, n], gh_r.at[1, n], up, c),
-            remote(ge.at[1, n], gcol.at[0, n], gh_s.at[2, n], gh_r.at[2, n], r, right),
-            remote(ge.at[0, n], gcol.at[1, n], gh_s.at[3, n], gh_r.at[3, n], r, left),
+            remote(gp.at[n, TILE], gp.at[n, 0], gh_s, gh_r.at[n], down, c),
+            remote(gp.at[n, 1], gp.at[n, TILE + 1], gh_s, gh_r.at[n], up, c),
+            remote(ge.at[1, n], gcol.at[0, n], gh_s, gh_r.at[n], r, right),
+            remote(ge.at[0, n], gcol.at[1, n], gh_s, gh_r.at[n], r, left),
         ]
         for k, (to_row, to_col) in enumerate(corners):
-            copies.append(
-                remote(gc.at[k, n], gcor.at[3 - k, n], gh_s.at[4 + k, n], gh_r.at[7 - k, n], to_row, to_col)
-            )
+            copies.append(remote(gc.at[k, n], gcor.at[3 - k, n], gh_s, gh_r.at[n], to_row, to_col))
         return copies
 
     def clear(pad, col, cor, n):
         count, at = (N_EX, slice(None)) if n is None else (1, pl.ds(n, 1))
         row_zero = jnp.zeros((count, 1, TILE, CH), BF16)
         col_zero = jnp.zeros((1, count, TILE, CH), BF16)
-        cor_zero = jnp.zeros((1, count, 16, CH), BF16)
+        cor_zero = jnp.zeros((1, N_EX, CH), F32) if n is None else jnp.zeros((1, 1, 16, CH), BF16)
 
         @pl.when(r == 0)
         def _():
@@ -150,14 +151,14 @@
             cor[1:2, at] = cor_zero
             cor[3:4, at] = cor_zero
 
-    def spread(pad, col, cor, n):
+    def spread(pad, col, spot, n):
         tile = wide.reshape(TILE + 2, PITCH, CH)
         tile[:, 8 : 8 + TILE, :] = pad[n].astype(F32)
         for side, slot in ((0, 7), (1, 8 + TILE)):
             wide[pl.ds(PITCH + slot, TILE, stride=PITCH), :] = col[side, n].astype(F32)
-            wide[slot : slot + 1, :] = cor[side, n].astype(F32)[0:1]
+            wide[slot : slot + 1, :] = spot(side)
             last = (TILE + 1) * PITCH + slot
-            wide[last : last + 1, :] = cor[2 + side, n].astype(F32)[0:1]
+            wide[last : last + 1, :] = spot(2 + side)
         taps[:, :, CH : 2 * CH] = pad[n]
         taps[:, :, 0:CH] = tile[:, 7 : 7 + TILE, :].astype(BF16)
         taps[:, :, 2 * CH :] = tile[:, 9 : 9 + TILE, :].astype(BF16)
@@ -172,21 +173,17 @@
         return total
 
     def core_copy(m):
-        return remote(stage.at[m, 1 - core], crx.at[m], c_s.at[m], c_r.at[m], mate, c)
+        return remote(stage.at[m, 1 - core], crx.at[m], c_s, c_r.at[m], mate, c)
 
     def y1_copy(m):
-        return remote(y1tx.at[m], y1rx.at[m], y1_s.at[m], y1_r.at[m], 2 * p1 + core, c)
+        return remote(y1tx.at[m], y1rx.at[m], y1_s, y1_r.at[m], 2 * p1 + core, c)
 
     def y2_copy(m):
-        return remote(y2tx.at[m], y2rx.at[m], y2_s.at[m], y2_r.at[m], 2 * p2 + core, c)
+        return remote(y2tx.at[m], y2rx.at[m], y2_s, y2_r.at[m], 2 * p2 + core, c)
 
     def z_copy(m, k):
         to = (c + k) % 8
-        return remote(zst.at[to, m], zrx.at[c, m], z_s.at[k, m], z_r.at[k, m], r, to)
-
-    def z_arrival(m, k):
-        src = (c + 8 - k) % 8
-        return remote(zst.at[src, m], zrx.at[src, m], z_s.at[k, m], z_r.at[k, m], r, src)
+        return remote(zst.at[to, m], zrx.at[c, m], z_s, z_r, r, to)
 
     def step_y1(m):
         core_copy(m).wait_recv()
@@ -218,18 +215,17 @@
 
     for copy in x_halo():
         copy.start()
-    for copy in x_halo():
-        copy.wait_recv()
+    received(x_bytes, xh_r)
     clear(xp, xcol, xcor, None)
+    load_cot.wait()
 
     def first(n, carry):
-        spread(xp, xcol, xcor, n)
-        load_cot(n).wait()
+        spread(xp, xcol, lambda k: xcor[k, pl.ds(n, 1), :], n)
         acc[...] = conv(w_ref)
-        z = acc[...] + b_ref[...]
-        s = 1.0 / (1.0 + jnp.exp(-z))
-        slope = s * (1.0 + z * (1.0 - s))
-        g = (cot[n].reshape(PIX, CH).astype(F32) * slope).astype(BF16)
+        half = 0.5 * (acc[...] + b_ref[...])
+        t = jnp.tanh(half)
+        slope = (1.0 + t) + half * (1.0 - t * t)
+        g = (0.5 * cot[n].reshape(PIX, CH).astype(F32) * slope).astype(BF16)
         gp[n, 1 : TILE + 1] = g.reshape(TILE, TILE, CH)
         wide_g = g.astype(F32)
         g32[...] = wide_g
@@ -270,22 +266,59 @@
     lax.fori_loop(0, N_EX, first, 0)
 
     def store_out(n):
-        return pltpu.make_async_copy(outb.at[n], out_hbm.at[n], lo_s.at[n])
+        return pltpu.make_async_copy(outb.at[n], out_hbm.at[n], lo_s)
+
+    def b1_copy(k):
+        return remote(b1st, b1rx.at[c], b1_s, b1_r, r, (c + k) % 8)
+
+    def b2_copy(k):
+        return remote(b2st, b2rx.at[r], b2_s, b2_r, (r + k) % 8, c)
+
+    def n1_copy(k):
+        return remote(n1st, n1rx.at[c], n1_s, n1_r, r, (c + k) % 8)
+
+    def n2_copy(k):
+        return remote(n2st, n2rx.at[r], n2_s, n2_r, (r + k) % 8, c)
+
+    def e_copy(k):
+        return remote(est, erx.at[e], e_s, e_r, r, c, (e + k) % 4)
+
+    away = (4, 3, 5, 2, 6, 1, 7)
+
+    def add_up(rx):
+        total = rx[0]
+        for k in range(1, 8):
+            total = total + rx[k]
+        return total
+
+    def bias_z(_):
+        for m in range(N_EX):
+            b1st[m : m + 1, :] = jnp.sum(bpart[m], axis=0, keepdims=True)
+        b1rx[c] = b1st[...]
+        for k in away:
+            b1_copy(k).start()
+
+    def bias_row(_):
+        received(b1rx.at[0:7], b1_r)
+        total = add_up(b1rx)
+        b2st[...] = total
+        b2rx[r] = total
+        for k in away:
+            b2_copy(k).start()
 
     plan = {
-        0: ((step_z, 3), (step_y2, 5)),
+        0: ((step_z, 3), (step_y2, 5), (bias_z, 0)),
         1: ((step_y1, 7),),
         2: ((step_z, 4), (step_y2, 6)),
         3: ((step_z, 5),),
-        5: ((step_z, 6), (step_y2, 7)),
+        5: ((step_z, 6), (step_y2, 7), (bias_row, 0)),
         7: ((step_z, 7),),
     }
 
     def second(n, carry):
-        for copy in g_halo(n):
-            copy.wait_recv()
+        received(gp.at[n, 0:6], gh_r.at[n])
         clear(gp, gcol, gcor, n)
-        spread(gp, gcol, gcor, n)
+        spread(gp, gcol, lambda k: gcor[k, n].astype(F32)[0:1], n)
         outb[n] = conv(wback).astype(BF16).reshape(TILE, TILE, CH)
         store_out(n).start()
         for when, steps in plan.items():
@@ -299,90 +332,61 @@
 
     lax.fori_loop(0, N_EX, second, 0)
 
+    received(b2rx.at[0:7], b2_r)
+    bias_sum = add_up(b2rx)
     keep = lax.broadcasted_iota(jnp.int32, (8, CH), 0) < OWN - 16
+    own_lane = lax.broadcasted_iota(jnp.int32, (8, CH), 1) // 16 == lax.broadcasted_iota(jnp.int32, (8, CH), 0)
+    received(zrx.at[0:7], z_r)
     for m in range(N_EX):
-        for k in range(1, 8):
-            z_arrival(m, k).wait_recv()
         total = zrx[0, m].astype(F32)
         for k in range(1, 8):
             total = total + zrx[k, m].astype(F32)
         zacc[m] = total[0:24]
         square = total * total
         part = square[0:8] + square[8:16] + jnp.where(keep, square[16:24], 0.0)
-        n1st[m : m + 1, :] = jnp.sum(part, axis=0, keepdims=True)
-        n1st[N_EX + m : N_EX + m + 1, :] = jnp.sum(bpart[m], axis=0, keepdims=True)
-
-    def n1_copy(k):
-        return remote(n1st, n1rx.at[c], n1_s.at[k], n1_r.at[k], r, (c + k) % 8)
-
-    def n1_arrival(k):
-        return remote(n1st, n1rx.at[(c + 8 - k) % 8], n1_s.at[k], n1_r.at[k], r, (c + 8 - k) % 8)
-
-    def n2_copy(k):
-        return remote(n2st, n2rx.at[r], n2_s.at[k], n2_r.at[k], (r + k) % 8, c)
-
-    def n2_arrival(k):
-        return remote(n2st, n2rx.at[(r + 8 - k) % 8], n2_s.at[k], n2_r.at[k], (r + 8 - k) % 8, c)
-
-    def e_copy(k):
-        return remote(est, erx.at[e], e_s.at[k], e_r.at[k], r, c, (e + k) % 4)
-
-    def e_arrival(k):
-        return remote(est, erx.at[(e + 4 - k) % 4], e_s.at[k], e_r.at[k], r, c, (e + 4 - k) % 4)
-
-    for k in (4, 3, 5, 2, 6, 1, 7):
+        fst[m : m + 1, :] = jnp.sum(part, axis=0, keepdims=True)
+    folded = fst[...]
+    for width in (64, 32, 16):
+        folded = folded + pltpu.roll(folded, width, 1)
+    total = jnp.sum(jnp.where(own_lane, folded, 0.0), axis=0, keepdims=True)
+    n1st[...] = total
+    n1rx[c] = total
+    for k in away:
         n1_copy(k).start()
-    n1rx[c] = n1st[...]
-    for k in range(1, 8):
-        n1_arrival(k).wait_recv()
-    total = n1rx[0]
-    for k in range(1, 8):
-        total = total + n1rx[k]
+    received(n1rx.at[0:7], n1_r)
+    total = add_up(n1rx)
     n2st[...] = total
-    for k in (4, 3, 5, 2, 6, 1, 7):
+    n2rx[r] = total
+    for k in away:
         n2_copy(k).start()
-    n2rx[r] = total
-    for k in range(1, 8):
-        n2_arrival(k).wait_recv()
-    total = n2rx[0]
-    for k in range(1, 8):
-        total = total + n2rx[k]
-    bias_sum = total[N_EX:]
-    squares = jnp.sum(total[0:N_EX] + bias_sum * bias_sum, axis=1, keepdims=True)
-    factor = jnp.minimum(1.0, clip / jnp.sqrt(squares + epsilon))
+    received(n2rx.at[0:7], n2_r)
+    total = add_up(n2rx)
+    squares = jnp.where(own_lane, jnp.broadcast_to(total, (N_EX, CH)), 0.0) + bias_sum * bias_sum
+    factor = jnp.minimum(1.0, clip / jnp.sqrt(jnp.sum(squares, axis=1, keepdims=True) + epsilon))
     fst[...] = jnp.broadcast_to(factor, (N_EX, CH))
     weighted = fst[0:1, :] * zacc[0]
     for m in range(1, N_EX):
         weighted = weighted + fst[m : m + 1, :] * zacc[m]
     est[...] = weighted
     est[OWN : OWN + 1, :] = jnp.sum(fst[...] * bias_sum, axis=0, keepdims=True)
+    erx[e] = est[...]
     for k in (2, 1, 3):
         e_copy(k).start()
-    erx[e] = est[...]
-    for k in range(1, 4):
-        e_arrival(k).wait_recv()
+    received(erx.at[0:3], e_r)
     sum_ref[...] = (erx[0] + erx[1]) + (erx[2] + erx[3])
 
-    for copy in x_halo():
-        copy.wait_send()
-
-    def drain(n, carry):
-        for copy in g_halo(n):
-            copy.wait_send()
-        core_copy(n).wait_send()
-        y1_copy(n).wait_send()
-        y2_copy(n).wait_send()
-        for k in range(1, 8):
-            z_copy(n, k).wait_send()
-        store_out(n).wait()
-        return carry
-
-    lax.fori_loop(0, N_EX, drain, 0)
-    for k in range(1, 8):
-        n1_copy(k).wait_send()
-        n2_copy(k).wait_send()
-    for k in range(1, 4):
-        e_copy(k).wait_send()
+    sent(x_bytes, xh_s)
+    sent(gp.at[:, 0:6], gh_s)
+    sent(crx, c_s)
+    sent(y1tx, y1_s)
+    sent(y2tx, y2_s)
+    sent(zst.at[0:7], z_s)
+    sent(b1rx.at[0:7], b1_s)
+    sent(b2rx.at[0:7], b2_s)
+    sent(n1rx.at[0:7], n1_s)
+    sent(n2rx.at[0:7], n2_s)
+    sent(erx.at[0:3], e_s)
+    pltpu.make_async_copy(outb, out_hbm, lo_s).wait()
 
 
 def local(inputs, cotangent, weight, bias, noise_weight, noise_bias):
@@ -393,6 +397,7 @@
     scale = 1.0 / math.sqrt(examples * lax.axis_size("ex") * height * width)
     vmem, anywhere = pl.BlockSpec(memory_space=pltpu.VMEM), pl.BlockSpec(memory_space=pl.ANY)
     halo_col, halo_cor = pltpu.VMEM((2, N_EX, TILE, CH), BF16), pltpu.VMEM((4, N_EX, 16, CH), BF16)
+    spots = pltpu.VMEM((4, N_EX, CH), F32)
     dma = pltpu.SemaphoreType.DMA
     input_grad, total = pl.pallas_call(
         functools.partial(kernel, clip),
@@ -405,12 +410,12 @@
         scratch_shapes=[
             pltpu.VMEM((3, 3 * CH, CH), BF16),
             pltpu.VMEM((1, CH), F32),
-            halo_col, halo_cor,
+            halo_col, spots,
             pltpu.VMEM((TILE * 16, CH), F32),
             pltpu.VMEM((N_EX, TILE + 2, TILE, CH), BF16),
             pltpu.VMEM((N_EX, TILE, TILE, CH), BF16),
             pltpu.VMEM((N_EX, TILE + 2, TILE, CH), BF16),
-            halo_col, halo_cor, halo_col, halo_cor, halo_col, halo_cor,
+            halo_col, spots, halo_col, halo_cor, halo_col, halo_cor,
             pltpu.VMEM(((TILE + 2) * PITCH, CH), F32),
             pltpu.VMEM((TILE + 2, TILE, 3 * CH), BF16),
             pltpu.VMEM((CH, PIX), BF16),
@@ -431,18 +436,21 @@
             pltpu.VMEM((8, N_EX, PIECE, CH), BF16),
             pltpu.VMEM((N_EX, 24, CH), F32),
             pltpu.VMEM((N_EX, 8, CH), F32),
-            pltpu.VMEM((2 * N_EX, CH), F32),
-            pltpu.VMEM((8, 2 * N_EX, CH), F32),
-            pltpu.VMEM((2 * N_EX, CH), F32),
-            pltpu.VMEM((8, 2 * N_EX, CH), F32),
+            pltpu.VMEM((N_EX, CH), F32),
+            pltpu.VMEM((8, N_EX, CH), F32),
+            pltpu.VMEM((N_EX, CH), F32),
+            pltpu.VMEM((8, N_EX, CH), F32),
+            pltpu.VMEM((1, CH), F32),
+            pltpu.VMEM((8, 1, CH), F32),
+            pltpu.VMEM((1, CH), F32),
+            pltpu.VMEM((8, 1, CH), F32),
             pltpu.VMEM((N_EX, CH), F32),
             pltpu.VMEM((24, CH), F32),
             pltpu.VMEM((4, 24, CH), F32),
-            dma((2,)), dma((N_EX,)), dma((N_EX,)), dma((N_EX,)),
-            dma((8,)), dma((8,)), dma((8, N_EX)), dma((8, N_EX)),
-            dma((N_EX,)), dma((N_EX,)), dma((N_EX,)), dma((N_EX,)), dma((N_EX,)), dma((N_EX,)),
-            dma((8, N_EX)), dma((8, N_EX)),
-            dma((8,)), dma((8,)), dma((8,)), dma((8,)), dma((4,)), dma((4,)),
+            dma((2,)), dma((N_EX,)), dma(()), dma(()),
+            dma(()), dma(()), dma(()), dma((N_EX,)),
+            dma(()), dma((N_EX,)), dma(()), dma((N_EX,)), dma(()), dma((N_EX,)), dma(()), dma(()),
+            dma(()), dma(()), dma(()), dma(()), dma(()), dma(()), dma(()), dma(()), dma(()), dma(()),
         ],
         compiler_params=pltpu.CompilerParams(
             collective_id=0, has_side_effects=True

time: 68.4 us -> 63.6 us (0.930)
  Pallas kernels: 61.8 us -> 56.9 us
    pallas_call x1, Pallas kernels: 61.8 us -> 56.9 us  [local(): pl.pallas_call(functools.partial(kernel, clip), out_shape=(jax.ShapeDtype...]
where the time goes in v3:
time: 63.6 us; the launch traced here: 63.4 us
  Pallas kernels  56.9 us (89%)
  local copies, waits for them, and re-layouts  3.28 us (5%)
  other arithmetic  2.51 us (4%)
  between operations  0.67 us (1%)
    pallas_call x1, Pallas kernels, local(): pl.pallas_call(functools.partial(kernel, clip), out_shape=(jax.ShapeDtype...  56.9 us
    unnamed x5, local copies, waits for them, and re-layouts  3.28 us
    mul x1, other arithmetic, local(): (total[0:OWN] + noise_multiplier * clip * noise_weight) * scale  1.31 us

profile of v3, /device:TPU:1, one launch (start us, length us, event | category | flops | bytes accessed | tf_op | source)
XLA Modules:
  0.0 63.4 jit_solution(17992956122105552348)
XLA Ops:
  0.6 0.0 copy-start.1
  0.6 0.0 copy-start
  0.7 56.9 %clipped_grad.1 = (bf16[8,32,32,128]{3,2,1,0:T(8,128)(2,1)}, f32[24,128]{1,0:T(8,128)}) custom-call(bf16[8,32,32,128]{3,2,1,0:T(8,128)(2,1)} %x_hbm.1, bf16[8,32,32,128]{3,2,1,0:T(8,128)(2,1)} %cot_hbm.1, bf16[3,384,128]{2,1,0:T(8,128)(2,1)} %bitcast.6, f32[1,128]{1,0:T(1,128)} %bitcast.7), custom_call_target="tpu_custom_call" | custom-call | tf_op jit(solution)/shard_map/clipped_grad/pallas_call | solution.py:402
  57.6 0.0 copy-done.1
  57.6 1.2 %fusion = f32[128]{0:T(128)} fusion(f32[128]{0:T(128)S(1)} %copy-done.1, f32[24,128]{1,0:T(8,128)} %get-tuple-element.6), kind=kLoop, calls=%fused_computation.2 | loop fusion | flops 384 | bytes 1536 | tf_op jit(solution)/shard_map/mul | solution.py:463
  58.8 0.0 copy-done
  58.8 1.3 %add_multiply_fusion = f32[18,128]{1,0:T(8,128)} fusion(f32[18,128]{1,0:T(8,128)S(1)} %copy-done, f32[24,128]{1,0:T(8,128)} %get-tuple-element.6), kind=kLoop, calls=%fused_computation | loop fusion | flops 6912 | bytes 27648 | tf_op jit(solution)/shard_map/mul | solution.py:462
  60.1 3.3 %copy.10 = bf16[8,32,32,128]{3,2,1,0:T(8,128)(2,1)} copy(bf16[8,32,32,128]{3,2,1,0:T(8,128)(2,1)} %get-tuple-element.10) | data formatting | bytes 4194304
Async XLA Ops:
  0.6 57.0 %copy-start.1 = (f32[128]{0:T(128)S(1)}, f32[128]{0:T(128)}, u32[]{:S(2)}) copy-start(f32[128]{0:T(128)} %param.11) | copy-start | bytes 1540
  0.6 58.1 %copy-start = (f32[18,128]{1,0:T(8,128)S(1)}, f32[18,128]{1,0:T(8,128)}, u32[]{:S(2)}) copy-start(f32[18,128]{1,0:T(8,128)} %param.10) | copy-start | bytes 27652

commit v4 on v3

--- a/solution.py
+++ b/solution.py
@@ -26,11 +26,11 @@
 def kernel(
     clip,
     x_hbm, cot_hbm, w_hbm, b_hbm,
-    out_hbm, sum_ref,
-    w_ref, b_ref, xe_ref, xc_ref, edge, xp, cot, gp, xcol, xcor, gcol, gcor, ge, gc, wide, taps, gt, g32, wback, acc, outb,
+    out_ref, sum_ref,
+    w_ref, b_ref, xe_ref, xc_ref, edge, xp, cot, gp, xcol, xcor, gcol, gcor, ge, gc, wide, taps, gt, g32, wback, acc,
     stage, crx, y1own, y1tx, y1rx, y2own, y2tx, y2rx, t32, zst, zrx, zacc, bpart,
     b1st, b1rx, b2st, b2rx, n1st, n1rx, n2st, n2rx, fst, est, erx,
-    lw_s, lx_s, lc_s, lo_s, xh_s, xh_r, gh_s, gh_r, c_s, c_r, y1_s, y1_r, y2_s, y2_r, z_s, z_r,
+    lw_s, lx_s, lc_s, xh_s, xh_r, gh_s, gh_r, c_s, c_r, y1_s, y1_r, y2_s, y2_r, z_s, z_r,
     b1_s, b1_r, b2_s, b2_r, n1_s, n1_r, n2_s, n2_r, e_s, e_r,
 ):
     e, r, c = lax.axis_index("ex"), lax.axis_index("row"), lax.axis_index("col")
@@ -77,6 +77,131 @@
     for k in range(1, 4):
         pl.semaphore_signal(barrier, inc=1, device_id=((e + k) % 4, r, c), device_id_type=pl.DeviceIdType.MESH)
 
+    pl.semaphore_wait(barrier, 21)
+
+    def x_rows():
+        return [
+            remote(x_hbm.at[:, TILE - 1], xp.at[:, 0], xh_s, xh_r, down, c),
+            remote(x_hbm.at[:, 0], xp.at[:, TILE + 1], xh_s, xh_r, up, c),
+        ]
+
+    def x_columns():
+        copies = [
+            remote(xe_ref.at[1], xcol.at[0], xh_s, xh_r, r, right),
+            remote(xe_ref.at[0], xcol.at[1], xh_s, xh_r, r, left),
+        ]
+        for k, (to_row, to_col) in enumerate(corners):
+            copies.append(remote(xc_ref.at[k], xcor.at[3 - k], xh_s, xh_r, to_row, to_col))
+        return copies
+
+    x_bytes = acc.at[0 : 4 * N_EX * TILE // 2 + 4 * N_EX]
+
+    def g_halo(n):
+        copies = [
+            remote(gp.at[n, TILE], gp.at[n, 0], gh_s, gh_r.at[n], down, c),
+            remote(gp.at[n, 1], gp.at[n, TILE + 1], gh_s, gh_r.at[n], up, c),
+            remote(ge.at[1, n], gcol.at[0, n], gh_s, gh_r.at[n], r, right),
+            remote(ge.at[0, n], gcol.at[1, n], gh_s, gh_r.at[n], r, left),
+        ]
+        for k, (to_row, to_col) in enumerate(corners):
+            copies.append(remote(gc.at[k, n], gcor.at[3 - k, n], gh_s, gh_r.at[n], to_row, to_col))
+        return copies
+
+    def clear(pad, col, cor, n):
+        count, at = (N_EX, slice(None)) if n is None else (1, pl.ds(n, 1))
+        row_zero = jnp.zeros((count, 1, TILE, CH), BF16)
+        col_zero = jnp.zeros((1, count, TILE, CH), BF16)
+        cor_zero = jnp.zeros((1, N_EX, CH), F32) if n is None else jnp.zeros((1, 1, 16, CH), BF16)
+
+        @pl.when(r == 0)
+        def _():
+            pad[at, 0:1] = row_zero
+            cor[0:1, at] = cor_zero
+            cor[1:2, at] = cor_zero
+
+        @pl.when(r == 7)
+        def _():
+            pad[at, TILE + 1 : TILE + 2] = row_zero
+            cor[2:3, at] = cor_zero
+            cor[3:4, at] = cor_zero
+
+        @pl.when(c == 0)
+        def _():
+            col[0:1, at] = col_zero
+            cor[0:1, at] = cor_zero
+            cor[2:3, at] = cor_zero
+
+        @pl.when(c == 7)
+        def _():
+            col[1:2, at] = col_zero
+            cor[1:2, at] = cor_zero
+            cor[3:4, at] = cor_zero
+
+    def spread(tap, pad, col, spot, n):
+        tile = wide.reshape(TILE + 2, PITCH, CH)
+        tile[:, 8 : 8 + TILE, :] = pad[n].astype(F32)
+        for side, slot in ((0, 7), (1, 8 + TILE)):
+            wide[pl.ds(PITCH + slot, TILE, stride=PITCH), :] = col[side, n].astype(F32)
+            wide[slot : slot + 1, :] = spot(side)
+            last = (TILE + 1) * PITCH + slot
+            wide[last : last + 1, :] = spot(2 + side)
+        tap[:, :, CH : 2 * CH] = pad[n]
+        tap[:, :, 0:CH] = tile[:, 7 : 7 + TILE, :].astype(BF16)
+        tap[:, :, 2 * CH :] = tile[:, 9 : 9 + TILE, :].astype(BF16)
+
+    def conv(tap, weights):
+        total = None
+        for a in range(3):
+            part = jnp.dot(
+                tap[a : a + TILE].reshape(PIX, 3 * CH), weights[a], preferred_element_type=F32
+            )
+            total = part if total is None else total + part
+        return total
+
+    def core_copy(m):
+        return remote(stage.at[m, 1 - core], crx.at[m], c_s, c_r.at[m], mate, c)
+
+    def y1_copy(m):
+        return remote(y1tx.at[m], y1rx.at[m], y1_s, y1_r.at[m], 2 * p1 + core, c)
+
+    def y2_copy(m):
+        return remote(y2tx.at[m], y2rx.at[m], y2_s, y2_r.at[m], 2 * p2 + core, c)
+
+    def z_copy(m, k):
+        to = (c + k) % 8
+        return remote(zst.at[to, m], zrx.at[c, m], z_s, z_r, r, to)
+
+    def step_y1(m):
+        core_copy(m).wait_recv()
+
+        def both(j):
+            return stage[m, core, j].astype(F32) + crx[m, j].astype(F32)
+
+        y1tx[m, 0] = both(p1).astype(BF16)
+        y1tx[m, 1] = both(far).astype(BF16)
+        y1_copy(m).start()
+        y1own[m, 0] = both(y)
+        y1own[m, 1] = both(p2)
+
+    def step_y2(m):
+        y1_copy(m).wait_recv()
+        y2tx[m] = (y1own[m, 1] + y1rx[m, 1].astype(F32)).astype(BF16)
+        y2_copy(m).start()
+        y2own[m] = y1own[m, 0] + y1rx[m, 0].astype(F32)
+
+    def step_z(m):
+        y2_copy(m).wait_recv()
+        t32[0:CHUNK, :] = y2own[m] + y2rx[m].astype(F32)
+        for k in range(8):
+            piece = t32[k * OWN : k * OWN + PIECE, :].astype(BF16)
+            zst[k, m] = piece
+        for k in range(1, 8):
+            z_copy(m, k).start()
+        zrx[c, m] = zst[c, m]
+
+    for copy in x_rows():
+        copy.start()
+
     def take_edges(n, carry):
         load_x(n).wait()
         for side in range(2):
@@ -89,139 +214,24 @@
         return carry
 
     lax.fori_loop(0, N_EX, take_edges, 0)
+    for copy in x_columns():
+        copy.start()
     load_w.wait()
     load_b.wait()
     for a in range(3):
         for b in range(3):
             wback[2 - a, (2 - b) * CH : (3 - b) * CH, :] = w_ref[a, b * CH : (b + 1) * CH, :].T
     t32[...] = jnp.zeros_like(t32)
-    pl.semaphore_wait(barrier, 21)
-
-    def x_halo():
-        copies = [
-            remote(x_hbm.at[:, TILE - 1], xp.at[:, 0], xh_s, xh_r, down, c),
-            remote(x_hbm.at[:, 0], xp.at[:, TILE + 1], xh_s, xh_r, up, c),
-            remote(xe_ref.at[1], xcol.at[0], xh_s, xh_r, r, right),
-            remote(xe_ref.at[0], xcol.at[1], xh_s, xh_r, r, left),
-        ]
-        for k, (to_row, to_col) in enumerate(corners):
-            copies.append(remote(xc_ref.at[k], xcor.at[3 - k], xh_s, xh_r, to_row, to_col))
-        return copies
-
-    x_bytes = acc.at[0 : 4 * N_EX * TILE // 2 + 4 * N_EX]
-
-    def g_halo(n):
-        copies = [
-            remote(gp.at[n, TILE], gp.at[n, 0], gh_s, gh_r.at[n], down, c),
-            remote(gp.at[n, 1], gp.at[n, TILE + 1], gh_s, gh_r.at[n], up, c),
-            remote(ge.at[1, n], gcol.at[0, n], gh_s, gh_r.at[n], r, right),
-            remote(ge.at[0, n], gcol.at[1, n], gh_s, gh_r.at[n], r, left),
-        ]
-        for k, (to_row, to_col) in enumerate(corners):
-            copies.append(remote(gc.at[k, n], gcor.at[3 - k, n], gh_s, gh_r.at[n], to_row, to_col))
-        return copies
-
-    def clear(pad, col, cor, n):
-        count, at = (N_EX, slice(None)) if n is None else (1, pl.ds(n, 1))
-        row_zero = jnp.zeros((count, 1, TILE, CH), BF16)
-        col_zero = jnp.zeros((1, count, TILE, CH), BF16)
-        cor_zero = jnp.zeros((1, N_EX, CH), F32) if n is None else jnp.zeros((1, 1, 16, CH), BF16)
-
-        @pl.when(r == 0)
-        def _():
-            pad[at, 0:1] = row_zero
-            cor[0:1, at] = cor_zero
-            cor[1:2, at] = cor_zero
-
-        @pl.when(r == 7)
-        def _():
-            pad[at, TILE + 1 : TILE + 2] = row_zero
-            cor[2:3, at] = cor_zero
-            cor[3:4, at] = cor_zero
-
-        @pl.when(c == 0)
-        def _():
-            col[0:1, at] = col_zero
-            cor[0:1, at] = cor_zero
-            cor[2:3, at] = cor_zero
-
-        @pl.when(c == 7)
-        def _():
-            col[1:2, at] = col_zero
-            cor[1:2, at] = cor_zero
-            cor[3:4, at] = cor_zero
-
-    def spread(pad, col, spot, n):
-        tile = wide.reshape(TILE + 2, PITCH, CH)
-        tile[:, 8 : 8 + TILE, :] = pad[n].astype(F32)
-        for side, slot in ((0, 7), (1, 8 + TILE)):
-            wide[pl.ds(PITCH + slot, TILE, stride=PITCH), :] = col[side, n].astype(F32)
-            wide[slot : slot + 1, :] = spot(side)
-            last = (TILE + 1) * PITCH + slot
-            wide[last : last + 1, :] = spot(2 + side)
-        taps[:, :, CH : 2 * CH] = pad[n]
-        taps[:, :, 0:CH] = tile[:, 7 : 7 + TILE, :].astype(BF16)
-        taps[:, :, 2 * CH :] = tile[:, 9 : 9 + TILE, :].astype(BF16)
-
-    def conv(weights):
-        total = None
-        for a in range(3):
-            part = jnp.dot(
-                taps[a : a + TILE].reshape(PIX, 3 * CH), weights[a], preferred_element_type=F32
-            )
-            total = part if total is None else total + part
-        return total
-
-    def core_copy(m):
-        return remote(stage.at[m, 1 - core], crx.at[m], c_s, c_r.at[m], mate, c)
-
-    def y1_copy(m):
-        return remote(y1tx.at[m], y1rx.at[m], y1_s, y1_r.at[m], 2 * p1 + core, c)
-
-    def y2_copy(m):
-        return remote(y2tx.at[m], y2rx.at[m], y2_s, y2_r.at[m], 2 * p2 + core, c)
-
-    def z_copy(m, k):
-        to = (c + k) % 8
-        return remote(zst.at[to, m], zrx.at[c, m], z_s, z_r, r, to)
-
-    def step_y1(m):
-        core_copy(m).wait_recv()
-
-        def both(j):
-            return stage[m, core, j].astype(F32) + crx[m, j].astype(F32)
-
-        y1tx[m, 0] = both(p1).astype(BF16)
-        y1tx[m, 1] = both(far).astype(BF16)
-        y1_copy(m).start()
-        y1own[m, 0] = both(y)
-        y1own[m, 1] = both(p2)
-
-    def step_y2(m):
-        y1_copy(m).wait_recv()
-        y2tx[m] = (y1own[m, 1] + y1rx[m, 1].astype(F32)).astype(BF16)
-        y2_copy(m).start()
-        y2own[m] = y1own[m, 0] + y1rx[m, 0].astype(F32)
-
-    def step_z(m):
-        y2_copy(m).wait_recv()
-        t32[0:CHUNK, :] = y2own[m] + y2rx[m].astype(F32)
-        for k in range(8):
-            piece = t32[k * OWN : k * OWN + PIECE, :].astype(BF16)
-            zst[k, m] = piece
-        for k in range(1, 8):
-            z_copy(m, k).start()
-        zrx[c, m] = zst[c, m]
-
-    for copy in x_halo():
-        copy.start()
     received(x_bytes, xh_r)
     clear(xp, xcol, xcor, None)
     load_cot.wait()
 
-    def first(n, carry):
-        spread(xp, xcol, lambda k: xcor[k, pl.ds(n, 1), :], n)
-        acc[...] = conv(w_ref)
+    def forward(n):
+        tap = taps.at[n % 2]
+        spread(tap, xp, xcol, lambda k: xcor[k, pl.ds(n, 1), :], n)
+        acc[...] = conv(tap, w_ref)
+
+    def output_grad(n):
         half = 0.5 * (acc[...] + b_ref[...])
         t = jnp.tanh(half)
         slope = (1.0 + t) + half * (1.0 - t * t)
@@ -234,39 +244,55 @@
         ge[1, n] = g32[pl.ds(TILE - 1, TILE, stride=TILE), :].astype(BF16)
         for k, at in enumerate((0, TILE - 1, PIX - TILE, PIX - 1)):
             gc[k, n] = jnp.broadcast_to(g32[at : at + 1, :], (16, CH)).astype(BF16)
+
+    def transpose_grad(n):
+        gt[...] = gp[n, 1 : TILE + 1].reshape(PIX, CH).T
+
+    def kernel_grad(n):
+        tap = taps.at[n % 2]
+        every = jnp.concatenate(
+            [tap[a : a + TILE].reshape(PIX, 3 * CH) for a in range(3)], axis=1
+        )
+        for start in range(0, ROWS, 2 * CH):
+            part = jnp.dot(gt[...], every[:, start : start + 2 * CH], preferred_element_type=F32)
+            for b in range(part.shape[1] // CH):
+                block = part[:, b * CH : (b + 1) * CH].T.astype(BF16)
+                for k in range(8):
+                    group = start // 16 + 8 * b + k
+                    owner, at = group // 9, group % 9 * 16
+                    stage[n, owner % 2, owner // 2, at : at + 16, :] = block[16 * k : 16 * k + 16]
+
+    def first(n, carry):
+        forward(n)
+        kernel_grad(n - 1)
+        output_grad(n)
+        transpose_grad(n)
         for copy in g_halo(n):
             copy.start()
-        gt[...] = gp[n, 1 : TILE + 1].reshape(PIX, CH).T
-        for a in range(3):
-            part = jnp.dot(
-                gt[...], taps[a : a + TILE].reshape(PIX, 3 * CH), preferred_element_type=F32
-            )
-            for b in range(3):
-                block = part[:, b * CH : (b + 1) * CH].T.astype(BF16)
-                for k in range(8):
-                    group = (3 * a + b) * 8 + k
-                    owner, at = group // 9, group % 9 * 16
-                    stage[n, owner % 2, owner // 2, at : at + 16, :] = block[16 * k : 16 * k + 16]
-        core_copy(n).start()
-
-        @pl.when(n >= 1)
-        def _():
-            step_y1(n - 1)
-
-        @pl.when(n >= 3)
-        def _():
-            step_y2(n - 3)
-
-        @pl.when(n >= 5)
-        def _():
-            step_z(n - 5)
+        core_copy(n - 1).start()
+
+        @pl.when(n >= 2)
+        def _():
+            step_y1(n - 2)
+
+        @pl.when(n >= 4)
+        def _():
+            step_y2(n - 4)
+
+        @pl.when(n >= 6)
+        def _():
+            step_z(n - 6)
 
         return carry
 
-    lax.fori_loop(0, N_EX, first, 0)
-
-    def store_out(n):
-        return pltpu.make_async_copy(outb.at[n], out_hbm.at[n], lo_s)
+    forward(0)
+    output_grad(0)
+    transpose_grad(0)
+    for copy in g_halo(0):
+        copy.start()
+    lax.fori_loop(1, N_EX, first, 0)
+    kernel_grad(N_EX - 1)
+    core_copy(N_EX - 1).start()
 
     def b1_copy(k):
         return remote(b1st, b1rx.at[c], b1_s, b1_r, r, (c + k) % 8)
@@ -307,20 +333,20 @@
             b2_copy(k).start()
 
     plan = {
-        0: ((step_z, 3), (step_y2, 5), (bias_z, 0)),
-        1: ((step_y1, 7),),
-        2: ((step_z, 4), (step_y2, 6)),
-        3: ((step_z, 5),),
-        5: ((step_z, 6), (step_y2, 7), (bias_row, 0)),
-        7: ((step_z, 7),),
+        0: ((step_z, 2), (step_y2, 4), (step_y1, 6)),
+        1: ((step_y1, 7), (bias_z, 0)),
+        2: ((step_y2, 5), (step_z, 3)),
+        3: ((step_z, 4),),
+        4: ((step_y2, 6), (step_y2, 7)),
+        5: ((step_z, 5), (bias_row, 0)),
+        7: ((step_z, 6), (step_z, 7)),
     }
 
     def second(n, carry):
         received(gp.at[n, 0:6], gh_r.at[n])
         clear(gp, gcol, gcor, n)
-        spread(gp, gcol, lambda k: gcor[k, n].astype(F32)[0:1], n)
-        outb[n] = conv(wback).astype(BF16).reshape(TILE, TILE, CH)
-        store_out(n).start()
+        spread(taps.at[0], gp, gcol, lambda k: gcor[k, n].astype(F32)[0:1], n)
+        out_ref[n] = conv(taps.at[0], wback).astype(BF16).reshape(TILE, TILE, CH)
         for when, steps in plan.items():
 
             @pl.when(n == when)
@@ -386,7 +412,6 @@
     sent(n1rx.at[0:7], n1_s)
     sent(n2rx.at[0:7], n2_s)
     sent(erx.at[0:3], e_s)
-    pltpu.make_async_copy(outb, out_hbm, lo_s).wait()
 
 
 def local(inputs, cotangent, weight, bias, noise_weight, noise_bias):
@@ -395,7 +420,7 @@
     width = tile_cols * lax.axis_size("col")
     clip = math.sqrt(height * width * 9 * channels * channels)
     scale = 1.0 / math.sqrt(examples * lax.axis_size("ex") * height * width)
-    vmem, anywhere = pl.BlockSpec(memory_space=pltpu.VMEM), pl.BlockSpec(memory_space=pl.ANY)
+    vmem, hbm = pl.BlockSpec(memory_space=pltpu.VMEM), pl.BlockSpec(memory_space=pltpu.MemorySpace.HBM)
     halo_col, halo_cor = pltpu.VMEM((2, N_EX, TILE, CH), BF16), pltpu.VMEM((4, N_EX, 16, CH), BF16)
     spots = pltpu.VMEM((4, N_EX, CH), F32)
     dma = pltpu.SemaphoreType.DMA
@@ -405,8 +430,8 @@
             jax.ShapeDtypeStruct(inputs.shape, BF16),
             jax.ShapeDtypeStruct((24, channels), F32),
         ),
-        in_specs=[pl.BlockSpec(memory_space=pltpu.MemorySpace.HBM)] * 4,
-        out_specs=[anywhere, vmem],
+        in_specs=[hbm] * 4,
+        out_specs=[vmem, vmem],
         scratch_shapes=[
             pltpu.VMEM((3, 3 * CH, CH), BF16),
             pltpu.VMEM((1, CH), F32),
@@ -417,12 +442,11 @@
             pltpu.VMEM((N_EX, TILE + 2, TILE, CH), BF16),
             halo_col, spots, halo_col, halo_cor, halo_col, halo_cor,
             pltpu.VMEM(((TILE + 2) * PITCH, CH), F32),
-            pltpu.VMEM((TILE + 2, TILE, 3 * CH), BF16),
+            pltpu.VMEM((2, TILE + 2, TILE, 3 * CH), BF16),
             pltpu.VMEM((CH, PIX), BF16),
             pltpu.VMEM((PIX, CH), F32),
             pltpu.VMEM((3, 3 * CH, CH), BF16),
             pltpu.VMEM((PIX, CH), F32),
-            pltpu.VMEM((N_EX, TILE, TILE, CH), BF16),
             pltpu.VMEM((N_EX, 2, 4, CHUNK, CH), BF16),
             pltpu.VMEM((N_EX, 4, CHUNK, CH), BF16),
             pltpu.VMEM((N_EX, 2, CHUNK, CH), F32),
@@ -447,17 +471,22 @@
             pltpu.VMEM((N_EX, CH), F32),
             pltpu.VMEM((24, CH), F32),
             pltpu.VMEM((4, 24, CH), F32),
-            dma((2,)), dma((N_EX,)), dma(()), dma(()),
+            dma((2,)), dma((N_EX,)), dma(()),
             dma(()), dma(()), dma(()), dma((N_EX,)),
             dma(()), dma((N_EX,)), dma(()), dma((N_EX,)), dma(()), dma((N_EX,)), dma(()), dma(()),
             dma(()), dma(()), dma(()), dma(()), dma(()), dma(()), dma(()), dma(()), dma(()), dma(()),
         ],
         compiler_params=pltpu.CompilerParams(
-            collective_id=0, has_side_effects=True
+            collective_id=0, has_side_effects=True, vmem_limit_bytes=48 * 2**20
         ),
         name="clipped_grad",
     )(
-        inputs, cotangent, weight.reshape(3, 3 * channels, channels), bias.reshape(1, channels)
+        *(
+            pltpu.with_memory_space_constraint(operand, pltpu.MemorySpace.HBM)
+            for operand in (
+                inputs, cotangent, weight.reshape(3, 3 * channels, channels), bias.reshape(1, channels)
+            )
+        )
     )
     grad_weight = (total[0:OWN] + noise_multiplier * clip * noise_weight) * scale
     grad_bias = (total[OWN] + noise_multiplier * clip * noise_bias) * scale

time: 63.6 us -> 57.6 us (0.906)
  Pallas kernels: 56.9 us -> 54.4 us
  local copies, waits for them, and re-layouts: 3.28 us -> 1.33 us
  other arithmetic: 2.51 us -> 1.12 us
    pallas_call x1, Pallas kernels: 56.9 us -> 54.4 us  [local(): pl.pallas_call(functools.partial(kernel, clip), out_shape=(jax.ShapeDtype...]
    unnamed x5, local copies, waits for them, and re-layouts: 3.28 us -> 1.33 us
    mul x1, other arithmetic: 1.31 us -> 0.6 us  [local(): (total[0:OWN] + noise_multiplier * clip * noise_weight) * scale]
    mul x1, other arithmetic: 1.2 us -> 0.52 us  [local(): grad_bias = (total[OWN] + noise_multiplier * clip * noise_bias) * scale]
where the time goes in v4:
time: 57.6 us
  Pallas kernels  54.4 us (94%)
  local copies, waits for them, and re-layouts  1.33 us (2%)
  other arithmetic  1.12 us (2%)
  between operations  0.67 us (1%)
    pallas_call x1, Pallas kernels, local(): pl.pallas_call(functools.partial(kernel, clip), out_shape=(jax.ShapeDtype...  54.4 us
    unnamed x5, local copies, waits for them, and re-layouts  1.33 us

profile of v4, /device:TPU:1, one launch (start us, length us, event | category | flops | bytes accessed | tf_op | source)
XLA Modules:
  0.0 57.6 jit_solution(6977882548580262566)
XLA Ops:
  0.6 0.0 copy-start.1
  0.6 0.0 copy-start
  0.7 54.4 %clipped_grad.1 = (bf16[8,32,32,128]{3,2,1,0:T(8,128)(2,1)S(1)}, f32[24,128]{1,0:T(8,128)S(1)}) custom-call(bf16[8,32,32,128]{3,2,1,0:T(8,128)(2,1)} %x_hbm.1, bf16[8,32,32,128]{3,2,1,0:T(8,128)(2,1)} %cot_hbm.1, bf16[3,384,128]{2,1,0:T(8,128)(2,1)} %bitcast.6, f32[1,128]{1,0:T(1,128)} %bitcast.7), custom_call_target="tpu_custom_call" | custom-call | tf_op jit(solution)/shard_map/clipped_grad/pallas_call | solution.py:427
  55.1 0.0 copy-done.1
  55.1 0.5 fusion
  55.6 0.0 copy-done
  55.6 0.6 %add_multiply_fusion = f32[18,128]{1,0:T(8,128)} fusion(f32[18,128]{1,0:T(8,128)S(1)} %copy-done, f32[24,128]{1,0:T(8,128)S(1)} %get-tuple-element.6), kind=kLoop, calls=%fused_computation | loop fusion | flops 6912 | bytes 27648 | tf_op jit(solution)/shard_map/mul | solution.py:491
  56.2 1.3 %copy.10 = bf16[8,32,32,128]{3,2,1,0:T(8,128)(2,1)} copy(bf16[8,32,32,128]{3,2,1,0:T(8,128)(2,1)S(1)} %get-tuple-element.10) | data formatting | bytes 4194304
Async XLA Ops:
  0.6 54.5 %copy-start.1 = (f32[128]{0:T(128)S(1)}, f32[128]{0:T(128)}, u32[]{:S(2)}) copy-start(f32[128]{0:T(128)} %param.11) | copy-start | bytes 1540
  0.6 55.0 %copy-start = (f32[18,128]{1,0:T(8,128)S(1)}, f32[18,128]{1,0:T(8,128)}, u32[]{:S(2)}) copy-start(f32[18,128]{1,0:T(8,128)} %param.10) | copy-start | bytes 27652

commit v5 on v4

--- a/solution.py
+++ b/solution.py
@@ -19,6 +19,7 @@
 PIX = TILE * TILE
 ROWS = 9 * CH
 CHUNK = ROWS // 8
+EARLY = 2
 OWN = CHUNK // 8
 PIECE = 32
 
@@ -79,22 +80,27 @@
 
     pl.semaphore_wait(barrier, 21)
 
-    def x_rows():
+    batches = ((0, EARLY), (EARLY, N_EX))
+
+    def x_rows(k):
+        some = pl.ds(batches[k][0], batches[k][1] - batches[k][0])
         return [
-            remote(x_hbm.at[:, TILE - 1], xp.at[:, 0], xh_s, xh_r, down, c),
-            remote(x_hbm.at[:, 0], xp.at[:, TILE + 1], xh_s, xh_r, up, c),
+            remote(x_hbm.at[some, TILE - 1], xp.at[some, 0], xh_s, xh_r.at[k], down, c),
+            remote(x_hbm.at[some, 0], xp.at[some, TILE + 1], xh_s, xh_r.at[k], up, c),
         ]
 
-    def x_columns():
+    def x_columns(k):
+        some = pl.ds(batches[k][0], batches[k][1] - batches[k][0])
         copies = [
-            remote(xe_ref.at[1], xcol.at[0], xh_s, xh_r, r, right),
-            remote(xe_ref.at[0], xcol.at[1], xh_s, xh_r, r, left),
+            remote(xe_ref.at[1, some], xcol.at[0, some], xh_s, xh_r.at[k], r, right),
+            remote(xe_ref.at[0, some], xcol.at[1, some], xh_s, xh_r.at[k], r, left),
         ]
-        for k, (to_row, to_col) in enumerate(corners):
-            copies.append(remote(xc_ref.at[k], xcor.at[3 - k], xh_s, xh_r, to_row, to_col))
+        for i, (to_row, to_col) in enumerate(corners):
+            copies.append(remote(xc_ref.at[k, i], xcor.at[k, 3 - i], xh_s, xh_r.at[k], to_row, to_col))
         return copies
 
-    x_bytes = acc.at[0 : 4 * N_EX * TILE // 2 + 4 * N_EX]
+    def x_bytes(examples, parts):
+        return acc.at[0 : 2 * TILE * examples + 4 * N_EX * parts]
 
     def g_halo(n):
         copies = [
@@ -107,35 +113,38 @@
             copies.append(remote(gc.at[k, n], gcor.at[3 - k, n], gh_s, gh_r.at[n], to_row, to_col))
         return copies
 
-    def clear(pad, col, cor, n):
-        count, at = (N_EX, slice(None)) if n is None else (1, pl.ds(n, 1))
+    def clear(pad, col, cor, at, count):
         row_zero = jnp.zeros((count, 1, TILE, CH), BF16)
         col_zero = jnp.zeros((1, count, TILE, CH), BF16)
-        cor_zero = jnp.zeros((1, N_EX, CH), F32) if n is None else jnp.zeros((1, 1, 16, CH), BF16)
+        cor_zero = jnp.zeros(cor.shape[1:], cor.dtype)
 
         @pl.when(r == 0)
         def _():
             pad[at, 0:1] = row_zero
-            cor[0:1, at] = cor_zero
-            cor[1:2, at] = cor_zero
+            cor[0] = cor_zero
+            cor[1] = cor_zero
 
         @pl.when(r == 7)
         def _():
             pad[at, TILE + 1 : TILE + 2] = row_zero
-            cor[2:3, at] = cor_zero
-            cor[3:4, at] = cor_zero
+            cor[2] = cor_zero
+            cor[3] = cor_zero
 
         @pl.when(c == 0)
         def _():
             col[0:1, at] = col_zero
-            cor[0:1, at] = cor_zero
-            cor[2:3, at] = cor_zero
+            cor[0] = cor_zero
+            cor[2] = cor_zero
 
         @pl.when(c == 7)
         def _():
             col[1:2, at] = col_zero
-            cor[1:2, at] = cor_zero
-            cor[3:4, at] = cor_zero
+            cor[1] = cor_zero
+            cor[3] = cor_zero
+
+    def clear_x(k):
+        begin, end = batches[k]
+        clear(xp, xcol, xcor.at[k], pl.ds(begin, end - begin), end - begin)
 
     def spread(tap, pad, col, spot, n):
         tile = wide.reshape(TILE + 2, PITCH, CH)
@@ -199,36 +208,39 @@
             z_copy(m, k).start()
         zrx[c, m] = zst[c, m]
 
-    for copy in x_rows():
-        copy.start()
-
-    def take_edges(n, carry):
+    for k in range(2):
+        for copy in x_rows(k):
+            copy.start()
+
+    def take_edges(k, n):
         load_x(n).wait()
         for side in range(2):
             block = xp[n, 1 : TILE + 1, side * 16 : side * 16 + 16, :].astype(F32)
             edge[...] = block.reshape(TILE * 16, CH)
             column = edge[pl.ds(15 * side, TILE, stride=16), :]
             xe_ref[side, n] = column.astype(BF16)
-            xc_ref[side, pl.ds(n, 1), :] = column[0:1]
-            xc_ref[2 + side, pl.ds(n, 1), :] = column[TILE - 1 : TILE]
-        return carry
-
-    lax.fori_loop(0, N_EX, take_edges, 0)
-    for copy in x_columns():
-        copy.start()
+            xc_ref[k, side, pl.ds(n, 1), :] = column[0:1]
+            xc_ref[k, 2 + side, pl.ds(n, 1), :] = column[TILE - 1 : TILE]
+
+    xc_ref[...] = jnp.zeros_like(xc_ref)
+    for k, (begin, end) in enumerate(batches):
+        lax.fori_loop(begin, end, lambda n, carry, k=k: (take_edges(k, n), carry)[1], 0)
+        for copy in x_columns(k):
+            copy.start()
     load_w.wait()
     load_b.wait()
     for a in range(3):
         for b in range(3):
             wback[2 - a, (2 - b) * CH : (3 - b) * CH, :] = w_ref[a, b * CH : (b + 1) * CH, :].T
     t32[...] = jnp.zeros_like(t32)
-    received(x_bytes, xh_r)
-    clear(xp, xcol, xcor, None)
     load_cot.wait()
+    received(x_bytes(EARLY, 1), xh_r.at[0])
+    clear_x(0)
 
     def forward(n):
         tap = taps.at[n % 2]
-        spread(tap, xp, xcol, lambda k: xcor[k, pl.ds(n, 1), :], n)
+        batch = 0 if isinstance(n, int) else (n + N_EX - EARLY) // N_EX
+        spread(tap, xp, xcol, lambda k: xcor[batch, k, pl.ds(n, 1), :], n)
         acc[...] = conv(tap, w_ref)
 
     def output_grad(n):
@@ -263,6 +275,11 @@
                     stage[n, owner % 2, owner // 2, at : at + 16, :] = block[16 * k : 16 * k + 16]
 
     def first(n, carry):
+        @pl.when(n == EARLY)
+        def _():
+            received(x_bytes(N_EX - EARLY, 1), xh_r.at[1])
+            clear_x(1)
+
         forward(n)
         kernel_grad(n - 1)
         output_grad(n)
@@ -344,7 +361,7 @@
 
     def second(n, carry):
         received(gp.at[n, 0:6], gh_r.at[n])
-        clear(gp, gcol, gcor, n)
+        clear(gp, gcol, gcor.at[:, n], pl.ds(n, 1), 1)
         spread(taps.at[0], gp, gcol, lambda k: gcor[k, n].astype(F32)[0:1], n)
         out_ref[n] = conv(taps.at[0], wback).astype(BF16).reshape(TILE, TILE, CH)
         for when, steps in plan.items():
@@ -401,7 +418,7 @@
     received(erx.at[0:3], e_r)
     sum_ref[...] = (erx[0] + erx[1]) + (erx[2] + erx[3])
 
-    sent(x_bytes, xh_s)
+    sent(x_bytes(N_EX, 2), xh_s)
     sent(gp.at[:, 0:6], gh_s)
     sent(crx, c_s)
     sent(y1tx, y1_s)
@@ -414,6 +431,14 @@
     sent(erx.at[0:3], e_s)
 
 
+def finish(clip, scale, grad_ref, sum_ref, nw_ref, nb_ref, out_hbm, gw_ref, gb_ref, sem):
+    store = pltpu.make_async_copy(grad_ref, out_hbm, sem)
+    store.start()
+    gw_ref[...] = (sum_ref[0:OWN] + noise_multiplier * clip * nw_ref[...]) * scale
+    gb_ref[...] = (sum_ref[OWN : OWN + 1] + noise_multiplier * clip * nb_ref[...]) * scale
+    store.wait()
+
+
 def local(inputs, cotangent, weight, bias, noise_weight, noise_bias):
     examples, tile_rows, tile_cols, channels = inputs.shape
     height = tile_rows * lax.axis_size("row")
@@ -422,7 +447,7 @@
     scale = 1.0 / math.sqrt(examples * lax.axis_size("ex") * height * width)
     vmem, hbm = pl.BlockSpec(memory_space=pltpu.VMEM), pl.BlockSpec(memory_space=pltpu.MemorySpace.HBM)
     halo_col, halo_cor = pltpu.VMEM((2, N_EX, TILE, CH), BF16), pltpu.VMEM((4, N_EX, 16, CH), BF16)
-    spots = pltpu.VMEM((4, N_EX, CH), F32)
+    spots = pltpu.VMEM((2, 4, N_EX, CH), F32)
     dma = pltpu.SemaphoreType.DMA
     input_grad, total = pl.pallas_call(
         functools.partial(kernel, clip),
@@ -472,7 +497,7 @@
             pltpu.VMEM((24, CH), F32),
             pltpu.VMEM((4, 24, CH), F32),
             dma((2,)), dma((N_EX,)), dma(()),
-            dma(()), dma(()), dma(()), dma((N_EX,)),
+            dma(()), dma((2,)), dma(()), dma((N_EX,)),
             dma(()), dma((N_EX,)), dma(()), dma((N_EX,)), dma(()), dma((N_EX,)), dma(()), dma(()),
             dma(()), dma(()), dma(()), dma(()), dma(()), dma(()), dma(()), dma(()), dma(()), dma(()),
         ],
@@ -488,9 +513,20 @@
             )
         )
     )
-    grad_weight = (total[0:OWN] + noise_multiplier * clip * noise_weight) * scale
-    grad_bias = (total[OWN] + noise_multiplier * clip * noise_bias) * scale
-    return input_grad, grad_weight, grad_bias
+    input_grad, grad_weight, grad_bias = pl.pallas_call(
+        functools.partial(finish, clip, scale),
+        out_shape=(
+            jax.ShapeDtypeStruct(inputs.shape, BF16),
+            jax.ShapeDtypeStruct(noise_weight.shape, F32),
+            jax.ShapeDtypeStruct((1, channels), F32),
+        ),
+        in_specs=[vmem] * 4,
+        out_specs=[hbm, vmem, vmem],
+        scratch_shapes=[dma(())],
+        compiler_params=pltpu.CompilerParams(vmem_limit_bytes=16 * 2**20),
+        name="finish",
+    )(input_grad, total, noise_weight, noise_bias.reshape(1, channels))
+    return input_grad, grad_weight, grad_bias.reshape(channels)
 
 
 def solution(mesh):

time: 57.6 us -> 56.3 us (0.977)
  local copies, waits for them, and re-layouts: 1.33 us -> 0.01 us
  Pallas kernels: 54.4 us -> 55.6 us
  other arithmetic: 1.12 us -> 0 us
    pallas_call x0 -> x1, Pallas kernels: none -> 1.93 us  [local(): pl.pallas_call(functools.partial(finish, clip, scale), out_shape=(jax.Sha...]
    unnamed x5 -> x4, local copies, waits for them, and re-layouts: 1.33 us -> 0.01 us
    mul x2 -> x0, other arithmetic: 1.12 us -> none  [the longest x1 0.6 us: local(): (total[0:OWN] + noise_multiplier * clip * noise_weight) * scale]
    pallas_call x1, Pallas kernels: 54.4 us -> 53.6 us  [local(): pl.pallas_call(functools.partial(kernel, clip), out_shape=(jax.ShapeDtype...]
where the time goes in v5:
time: 56.3 us
  Pallas kernels  55.6 us (99%)
  between operations  0.67 us (1%)
    pallas_call x1, Pallas kernels, local(): pl.pallas_call(functools.partial(kernel, clip), out_shape=(jax.ShapeDtype...  53.6 us
    pallas_call x1, Pallas kernels, local(): pl.pallas_call(functools.partial(finish, clip, scale), out_shape=(jax.Sha...  1.93 us

profile of v5, /device:TPU:1, one launch (start us, length us, event | category | flops | bytes accessed | tf_op | source)
XLA Modules:
  0.0 56.3 jit_solution(1566084702027672791)
XLA Ops:
  0.6 0.0 copy-start
  0.6 0.0 copy-start.1
  0.7 53.6 %clipped_grad.1 = (bf16[8,32,32,128]{3,2,1,0:T(8,128)(2,1)S(1)}, f32[24,128]{1,0:T(8,128)S(1)}) custom-call(bf16[8,32,32,128]{3,2,1,0:T(8,128)(2,1)} %x_hbm.1, bf16[8,32,32,128]{3,2,1,0:T(8,128)(2,1)} %cot_hbm.1, bf16[3,384,128]{2,1,0:T(8,128)(2,1)} %bitcast.5, f32[1,128]{1,0:T(1,128)} %bitcast.6), custom_call_target="tpu_custom_call" | custom-call | tf_op jit(solution)/shard_map/clipped_grad/pallas_call | solution.py:452
  54.3 0.0 copy-done
  54.3 0.0 copy-done.1
  54.3 1.9 %finish.1 = (bf16[8,32,32,128]{3,2,1,0:T(8,128)(2,1)}, f32[18,128]{1,0:T(8,128)}, f32[1,128]{1,0:T(1,128)}) custom-call(bf16[8,32,32,128]{3,2,1,0:T(8,128)(2,1)S(1)} %get-tuple-element.8.grad_ref, f32[24,128]{1,0:T(8,128)S(1)} %get-tuple-element.9.sum_ref, f32[18,128]{1,0:T(8,128)S(1)} %copy-done, f32[1,128]{1,0:T(1,128)S(1)} %bitcast.4), custom_call_target="tpu_custom_call" | custom-call | tf_op jit(solution)/shard_map/finish/pallas_call | solution.py:516
Async XLA Ops:
  0.6 53.7 %copy-start = (f32[18,128]{1,0:T(8,128)S(1)}, f32[18,128]{1,0:T(8,128)}, u32[]{:S(2)}) copy-start(f32[18,128]{1,0:T(8,128)} %nw_ref.1) | copy-start | bytes 27652
  0.6 53.7 %copy-start.1 = (f32[128]{0:T(128)S(1)}, f32[128]{0:T(128)}, u32[]{:S(2)}) copy-start(f32[128]{0:T(128)} %param.11) | copy-start | bytes 1540

commit v6 on v5

--- a/solution.py
+++ b/solution.py
@@ -60,6 +60,15 @@
     def load_x(n):
         return pltpu.make_async_copy(x_hbm.at[n], xp.at[n, 1 : TILE + 1], lx_s.at[n])
 
+    barrier = pltpu.get_barrier_semaphore()
+    partners = list(corners)
+    partners += [((r + k) % 8, c) for k in range(1, 8)]
+    partners += [(r, (c + k) % 8) for k in range(1, 8)]
+    for to_row, to_col in partners:
+        pl.semaphore_signal(barrier, inc=1, device_id=(e, to_row, to_col), device_id_type=pl.DeviceIdType.MESH)
+    for k in range(1, 4):
+        pl.semaphore_signal(barrier, inc=1, device_id=((e + k) % 4, r, c), device_id_type=pl.DeviceIdType.MESH)
+
     load_w = pltpu.make_async_copy(w_hbm, w_ref, lw_s.at[0])
     load_b = pltpu.make_async_copy(b_hbm, b_ref, lw_s.at[1])
     for n in range(N_EX):
@@ -68,15 +77,6 @@
     load_b.start()
     load_cot = pltpu.make_async_copy(cot_hbm, cot, lc_s)
     load_cot.start()
-
-    barrier = pltpu.get_barrier_semaphore()
-    partners = list(corners)
-    partners += [((r + k) % 8, c) for k in range(1, 8)]
-    partners += [(r, (c + k) % 8) for k in range(1, 8)]
-    for to_row, to_col in partners:
-        pl.semaphore_signal(barrier, inc=1, device_id=(e, to_row, to_col), device_id_type=pl.DeviceIdType.MESH)
-    for k in range(1, 4):
-        pl.semaphore_signal(barrier, inc=1, device_id=((e + k) % 4, r, c), device_id_type=pl.DeviceIdType.MESH)
 
     pl.semaphore_wait(barrier, 21)
 
@@ -204,7 +204,7 @@
         for k in range(8):
             piece = t32[k * OWN : k * OWN + PIECE, :].astype(BF16)
             zst[k, m] = piece
-        for k in range(1, 8):
+        for k in (4, 3, 5, 2, 6, 1, 7):
             z_copy(m, k).start()
         zrx[c, m] = zst[c, m]
 
@@ -350,13 +350,14 @@
             b2_copy(k).start()
 
     plan = {
-        0: ((step_z, 2), (step_y2, 4), (step_y1, 6)),
-        1: ((step_y1, 7), (bias_z, 0)),
-        2: ((step_y2, 5), (step_z, 3)),
-        3: ((step_z, 4),),
-        4: ((step_y2, 6), (step_y2, 7)),
-        5: ((step_z, 5), (bias_row, 0)),
-        7: ((step_z, 6), (step_z, 7)),
+        0: ((step_z, 2), (step_y2, 4), (step_y1, 6), (bias_z, 0),),
+        1: ((step_y1, 7), (step_z, 3),),
+        2: ((step_y2, 5),),
+        3: ((step_y2, 6), (step_z, 4),),
+        4: ((step_y2, 7),),
+        5: ((step_z, 5),),
+        6: ((step_z, 6),),
+        7: ((step_z, 7), (bias_row, 0),),
     }
 
     def second(n, carry):
@@ -375,8 +376,6 @@
 
     lax.fori_loop(0, N_EX, second, 0)
 
-    received(b2rx.at[0:7], b2_r)
-    bias_sum = add_up(b2rx)
     keep = lax.broadcasted_iota(jnp.int32, (8, CH), 0) < OWN - 16
     own_lane = lax.broadcasted_iota(jnp.int32, (8, CH), 1) // 16 == lax.broadcasted_iota(jnp.int32, (8, CH), 0)
     received(zrx.at[0:7], z_r)
@@ -396,6 +395,8 @@
     n1rx[c] = total
     for k in away:
         n1_copy(k).start()
+    received(b2rx.at[0:7], b2_r)
+    bias_sum = add_up(b2rx)
     received(n1rx.at[0:7], n1_r)
     total = add_up(n1rx)
     n2st[...] = total
@@ -431,12 +432,18 @@
     sent(erx.at[0:3], e_s)
 
 
-def finish(clip, scale, grad_ref, sum_ref, nw_ref, nb_ref, out_hbm, gw_ref, gb_ref, sem):
-    store = pltpu.make_async_copy(grad_ref, out_hbm, sem)
-    store.start()
+def finish(clip, scale, grad_ref, sum_ref, nw_ref, nb_ref, out_hbm, gw_hbm, gb_hbm, gw_ref, gb_ref, sems):
+    stores = [pltpu.make_async_copy(grad_ref.at[n], out_hbm.at[n], sems.at[n]) for n in range(N_EX)]
+    stores.append(pltpu.make_async_copy(gw_ref, gw_hbm, sems.at[N_EX]))
+    stores.append(pltpu.make_async_copy(gb_ref, gb_hbm, sems.at[N_EX + 1]))
+    for store in stores[:N_EX]:
+        store.start()
     gw_ref[...] = (sum_ref[0:OWN] + noise_multiplier * clip * nw_ref[...]) * scale
     gb_ref[...] = (sum_ref[OWN : OWN + 1] + noise_multiplier * clip * nb_ref[...]) * scale
-    store.wait()
+    for store in stores[N_EX:]:
+        store.start()
+    for store in stores:
+        store.wait()
 
 
 def local(inputs, cotangent, weight, bias, noise_weight, noise_bias):
@@ -521,8 +528,10 @@
             jax.ShapeDtypeStruct((1, channels), F32),
         ),
         in_specs=[vmem] * 4,
-        out_specs=[hbm, vmem, vmem],
-        scratch_shapes=[dma(())],
+        out_specs=[hbm] * 3,
+        scratch_shapes=[
+            pltpu.VMEM(noise_weight.shape, F32), pltpu.VMEM((1, channels), F32), dma((N_EX + 2,))
+        ],
         compiler_params=pltpu.CompilerParams(vmem_limit_bytes=16 * 2**20),
         name="finish",
     )(input_grad, total, noise_weight, noise_bias.reshape(1, channels))

time: 56.3 us -> 54.9 us (0.975)
  Pallas kernels: 55.6 us -> 54.2 us
    pallas_call x1, Pallas kernels: 53.6 us -> 52.8 us  [local(): pl.pallas_call(functools.partial(kernel, clip), out_shape=(jax.ShapeDtype...]
where the time goes in v6:
time: 54.9 us; the launch traced here: 54.8 us
  Pallas kernels  54.2 us (99%)
  between operations  0.67 us (1%)
    pallas_call x1, Pallas kernels, local(): pl.pallas_call(functools.partial(kernel, clip), out_shape=(jax.ShapeDtype...  52.8 us
    pallas_call x1, Pallas kernels, local(): pl.pallas_call(functools.partial(finish, clip, scale), out_shape=(jax.Sha...  1.4 us

profile of v6, /device:TPU:1, one launch (start us, length us, event | category | flops | bytes accessed | tf_op | source)
XLA Modules:
  0.0 54.8 jit_solution(1818718885915465024)
XLA Ops:
  0.6 0.0 copy-start
  0.6 0.0 copy-start.1
  0.7 52.8 %clipped_grad.1 = (bf16[8,32,32,128]{3,2,1,0:T(8,128)(2,1)S(1)}, f32[24,128]{1,0:T(8,128)S(1)}) custom-call(bf16[8,32,32,128]{3,2,1,0:T(8,128)(2,1)} %x_hbm.1, bf16[8,32,32,128]{3,2,1,0:T(8,128)(2,1)} %cot_hbm.1, bf16[3,384,128]{2,1,0:T(8,128)(2,1)} %bitcast.5, f32[1,128]{1,0:T(1,128)} %bitcast.6), custom_call_target="tpu_custom_call" | custom-call | tf_op jit(solution)/shard_map/clipped_grad/pallas_call | solution.py:459
  53.4 0.0 copy-done
  53.4 0.0 copy-done.1
  53.4 1.4 %finish.1 = (bf16[8,32,32,128]{3,2,1,0:T(8,128)(2,1)}, f32[18,128]{1,0:T(8,128)}, f32[1,128]{1,0:T(1,128)}) custom-call(bf16[8,32,32,128]{3,2,1,0:T(8,128)(2,1)S(1)} %get-tuple-element.8.grad_ref, f32[24,128]{1,0:T(8,128)S(1)} %get-tuple-element.9.sum_ref, f32[18,128]{1,0:T(8,128)S(1)} %copy-done, f32[1,128]{1,0:T(1,128)S(1)} %bitcast.4), custom_call_target="tpu_custom_call" | custom-call | tf_op jit(solution)/shard_map/finish/pallas_call | solution.py:523
Async XLA Ops:
  0.6 52.8 %copy-start = (f32[18,128]{1,0:T(8,128)S(1)}, f32[18,128]{1,0:T(8,128)}, u32[]{:S(2)}) copy-start(f32[18,128]{1,0:T(8,128)} %nw_ref.1) | copy-start | bytes 27652
  0.6 52.8 %copy-start.1 = (f32[128]{0:T(128)S(1)}, f32[128]{0:T(128)}, u32[]{:S(2)}) copy-start(f32[128]{0:T(128)} %param.11) | copy-start | bytes 1540

commit v7 on v6

--- a/solution.py
+++ b/solution.py
@@ -19,7 +19,7 @@
 PIX = TILE * TILE
 ROWS = 9 * CH
 CHUNK = ROWS // 8
-EARLY = 2
+EARLY = 1
 OWN = CHUNK // 8
 PIECE = 32
 

time: 54.9 us -> 54.8 us (level)
  no operation moved by 1% of the time
where the time goes in v7:
time: 54.8 us; the launch traced here: 54.7 us
  Pallas kernels  54 us (99%)
  between operations  0.67 us (1%)
    pallas_call x1, Pallas kernels, local(): pl.pallas_call(functools.partial(kernel, clip), out_shape=(jax.ShapeDtype...  52.6 us
    pallas_call x1, Pallas kernels, local(): pl.pallas_call(functools.partial(finish, clip, scale), out_shape=(jax.Sha...  1.4 us

profile of v7, /device:TPU:1, one launch (start us, length us, event | category | flops | bytes accessed | tf_op | source)
XLA Modules:
  0.0 54.7 jit_solution(6904590959011511274)
XLA Ops:
  0.6 0.0 copy-start
  0.6 0.0 copy-start.1
  0.7 52.6 %clipped_grad.1 = (bf16[8,32,32,128]{3,2,1,0:T(8,128)(2,1)S(1)}, f32[24,128]{1,0:T(8,128)S(1)}) custom-call(bf16[8,32,32,128]{3,2,1,0:T(8,128)(2,1)} %x_hbm.1, bf16[8,32,32,128]{3,2,1,0:T(8,128)(2,1)} %cot_hbm.1, bf16[3,384,128]{2,1,0:T(8,128)(2,1)} %bitcast.5, f32[1,128]{1,0:T(1,128)} %bitcast.6), custom_call_target="tpu_custom_call" | custom-call | tf_op jit(solution)/shard_map/clipped_grad/pallas_call | solution.py:459
  53.3 0.0 copy-done
  53.3 0.0 copy-done.1
  53.3 1.4 %finish.1 = (bf16[8,32,32,128]{3,2,1,0:T(8,128)(2,1)}, f32[18,128]{1,0:T(8,128)}, f32[1,128]{1,0:T(1,128)}) custom-call(bf16[8,32,32,128]{3,2,1,0:T(8,128)(2,1)S(1)} %get-tuple-element.8.grad_ref, f32[24,128]{1,0:T(8,128)S(1)} %get-tuple-element.9.sum_ref, f32[18,128]{1,0:T(8,128)S(1)} %copy-done, f32[1,128]{1,0:T(1,128)S(1)} %bitcast.4), custom_call_target="tpu_custom_call" | custom-call | tf_op jit(solution)/shard_map/finish/pallas_call | solution.py:523
Async XLA Ops:
  0.6 52.6 %copy-start = (f32[18,128]{1,0:T(8,128)S(1)}, f32[18,128]{1,0:T(8,128)}, u32[]{:S(2)}) copy-start(f32[18,128]{1,0:T(8,128)} %nw_ref.1) | copy-start | bytes 27652
  0.6 52.6 %copy-start.1 = (f32[128]{0:T(128)S(1)}, f32[128]{0:T(128)}, u32[]{:S(2)}) copy-start(f32[128]{0:T(128)} %param.11) | copy-start | bytes 1540
